TPU v7x, 32 devices: a whole 2x2x4 slice. The times are simulated.
32 devices in a mesh: wide: 8 (over z, y), narrow: 4 (over x, core).
Axes of the slice: x: 2, y: 2, z: 4, core: 2. Of those that a mesh axis runs over, the one named last changes fastest.
Arguments:
- left_edge: bfloat16 [448, 49, 448], P('wide', None, 'narrow'), may hold values from -40 to 40
- corner: bfloat16 [448, 448], P('narrow'), may hold values from -0.25 to 0.25
- right_edge: bfloat16 [448, 49, 448], P('wide', None, 'narrow'), may hold values from -0.25 to 0.25
- single_layer: bfloat16 [2, 2401], replicated, may hold values from -0.71875 to 0.71875
- warm_basis: bfloat16 [49, 448, 448], P(None, 'narrow', 'wide'), may hold values from -0.0390625 to 0.0390625
Outputs:
- new_basis: float32 [448, 49, 448], P('wide', None, 'narrow')
- r_factor: float32 [448, 448], replicated
All inputs are finite; a program needn't handle non-finite values.
Results may differ from a plain program's by a relative error of at most 0.014.
Values may be sent and summed in bfloat16 or wider, within the bound.
No kernel may reach another device: no remote copies, remote signals or barrier semaphores. Data moves between devices by JAX's collectives and lax.ppermute only.
A program may use at most 192 MiB of HBM per device.

v0:
```python
import functools
import jax
import jax.numpy as jnp
from jax import lax
from jax.experimental import pallas as pl
from jax.experimental.pallas import tpu as pltpu
from jax.sharding import PartitionSpec as P


BOND = 7
LANES = 128
BLOCK = 128
PANEL = 8
ROWS = 512
OUTER = ROWS // 64
SPLIT = 7
F32 = jnp.float32
BF16 = jnp.bfloat16
HIGHEST = lax.Precision.HIGHEST


def site_operands(single_layer):
    phys = single_layer.shape[0]
    layer = single_layer.reshape(phys, BOND, BOND, BOND, BOND)
    half = 4
    padded = jnp.pad(layer, ((0, 0), (0, 1), (0, 0), (0, 0), (0, 0)))
    eye = jnp.eye(half, dtype=layer.dtype)
    first = padded.transpose(3, 4, 0, 2, 1)[:, :, :, None, :, None, :] * eye[None, None, None, :, None, :, None]
    first = first.reshape(BOND * BOND * phys * half, BOND * half * 8)
    split = padded.reshape(phys, 2, half, BOND, BOND, BOND)
    second = jnp.pad(split.transpose(5, 4, 3, 1, 0, 2), ((0, 0), (0, 1), (0, 0), (0, 0), (0, 0), (0, 0)))
    return first, second.reshape(BOND * 8, BOND * 2 * phys * half)


def assemble(layout, order_ref, pieces, stage, target, sems):
    copies = [pltpu.make_async_copy(piece, stage.at[block, pl.ds(begin, size)], sems.at[s])
              for s, ((block, begin, size), piece) in enumerate(zip(layout, pieces))]
    for copy in copies:
        copy.start()
    target[...] = jnp.zeros_like(target)
    for copy in copies:
        copy.wait()
    count, square, depth, breadth = stage.shape

    def fill(q, carry):
        lane = pl.ds(pl.multiple_of(q * LANES, LANES), breadth)
        if count == 1:
            target[:, lane] = stage[0, q]
        for pair in range(count // 2):
            joined = jnp.concatenate(
                [stage[order_ref[2 * pair + k], q].astype(F32) for k in range(2)], axis=0)
            target[pl.ds(pair * 2 * depth, 2 * depth), lane] = joined.astype(BF16)
        return carry

    lax.fori_loop(0, square, fill, 0)


def half_left_kernel(parts_of, *refs):
    left_refs, corner_refs = refs[:parts_of], refs[parts_of:2 * parts_of]
    out_ref, total, spread = refs[2 * parts_of:]
    value = jnp.dot(left_refs[0][...], corner_refs[0][...], preferred_element_type=F32)
    for n in range(1, parts_of):
        value += jnp.dot(left_refs[n][...], corner_refs[n][...], preferred_element_type=F32)
    outer = total.shape[0] // (BOND * BOND)
    spread[...] = jnp.zeros_like(spread)
    width = value.shape[1]
    total[:, :width] = value

    def place(u, v):
        begin = (u * BOND + v) * outer
        if outer % 8 == 0:
            begin = pl.multiple_of(begin, 8)
        for c in range(spread.shape[0]):
            data = total[pl.ds(begin, outer), c * LANES:(c + 1) * LANES]
            spread[c, pl.ds(v * 8 + u, outer, stride=64), :] = data

    if outer % 8 == 0:
        lax.fori_loop(0, BOND * BOND, lambda p, carry: (place(p // BOND, p % BOND), carry)[1], 0)
    else:
        for p in range(BOND * BOND):
            place(p // BOND, p % BOND)
    for c in range(spread.shape[0]):
        count = min(LANES, width - c * LANES)
        out_ref[:, c * LANES:c * LANES + count] = spread[c, :, :count].astype(BF16)


def half_left_of(lefts, corners, outer):
    width = corners[0].shape[1]
    return pl.pallas_call(
        functools.partial(half_left_kernel, len(lefts)),
        out_shape=jax.ShapeDtypeStruct((outer * 64, width), BF16),
        scratch_shapes=[pltpu.VMEM((lefts[0].shape[0], -(-width // LANES) * LANES), F32),
                        pltpu.VMEM((-(-width // LANES), outer * 64, LANES), F32)],
        compiler_params=pltpu.CompilerParams(vmem_limit_bytes=60 << 20),
        name="half_left",
    )(*lefts, *corners)


def enlarge_kernel(layout, order_ref, half_ref, first_ref, second_ref, *rest):
    count = len(layout)
    if count:
        pieces, (out_ref, right_all, stage, strip, ket, sems) = rest[:count], rest[count:]

        @pl.when(pl.program_id(0) == 0)
        def _():
            assemble(layout, order_ref, pieces, stage, right_all, sems)
    else:
        right_all, _, out_ref, strip, ket = rest
    rows = half_ref.shape[0]
    square = BOND * BOND
    span = BOND * LANES
    half_left = half_ref[...]
    for l in range(BOND):
        strip[l] = jnp.dot(half_left, right_all[:, l * span:(l + 1) * span], preferred_element_type=F32).astype(BF16)

    def one_pair(pair, carry):
        for i in range(2):
            parts = []
            for g in range(2):
                at = pl.ds(pl.multiple_of((pair * 2 + i) * 64 + g * 32, 32), 32)
                data = strip[:, at, :].reshape(BOND * 32, span)
                part = jnp.dot(first_ref[...], data, preferred_element_type=F32)
                parts.append(part.reshape(square, 8, span))
            ket[i] = jnp.concatenate(parts, axis=1).astype(BF16)
        for d in range(BOND):
            rows_of = []
            for lp in range(BOND):
                rows_of.append(jnp.concatenate(
                    [ket[i, d * BOND + r, :, lp * LANES:(lp + 1) * LANES] for r in range(BOND) for i in range(2)],
                    axis=1))
            data = jnp.concatenate(rows_of, axis=0)
            value = jnp.dot(second_ref[...], data, preferred_element_type=F32)
            at = pl.ds(pl.multiple_of((pair * BOND + d) * 16, 16), 16)
            for r in range(BOND):
                two = [value[:, (r * 2 + i) * LANES:(r * 2 + i + 1) * LANES].reshape(BOND, 8, LANES)
                       for i in range(2)]
                both = jnp.concatenate(two, axis=1).astype(BF16)
                for rp in range(BOND):
                    out_ref[at, (r * BOND + rp) * LANES:(r * BOND + rp + 1) * LANES] = both[rp]
        return carry

    lax.fori_loop(0, rows // 128, one_pair, 0)


def whole_block(a):
    return pl.BlockSpec(a.shape, lambda s: (0,) * a.ndim, pipeline_mode=pl.Buffered(1))


def shape_of(pieces):
    blocks = 1 + max(block for block, _, _ in pieces)
    square = sum(piece.shape[0] for block, _, piece in pieces if block == 0)
    return (blocks, square) + pieces[0][2].shape[1:]


def layout_of(pieces):
    return tuple((block, begin, piece.shape[0]) for block, begin, piece in pieces)


def enlarge(half_left, right, order, first, second, begin, steps, before=None):
    total, depth = half_left.shape
    pieces = right if isinstance(right, list) else None
    square = BOND * BOND
    lanes = square * LANES
    out_rows = ROWS // 128 * BOND * 16
    in_specs = [pl.BlockSpec(memory_space=pltpu.SMEM), pl.BlockSpec((ROWS, depth), lambda s: (s + begin, 0)),
                whole_block(first), whole_block(second)]
    out_specs = [pl.BlockSpec((out_rows, lanes), lambda s: (s + begin, 0))]
    out_shape = [jax.ShapeDtypeStruct((total // ROWS * out_rows, lanes), BF16)]
    scratch = [pltpu.VMEM((BOND, ROWS, BOND * LANES), BF16), pltpu.VMEM((2, square, 16, BOND * LANES), BF16)]
    if pieces:
        shape = shape_of(pieces)
        width = shape[0] * shape[2]
        in_specs += [pl.BlockSpec(memory_space=pl.ANY)] * len(pieces)
        out_specs.append(pl.BlockSpec((width, lanes), lambda s: (0, 0), pipeline_mode=pl.Buffered(1)))
        out_shape.append(jax.ShapeDtypeStruct((width, lanes), BF16))
        scratch = [pltpu.VMEM(shape, BF16)] + scratch
        scratch.append(pltpu.SemaphoreType.DMA((len(pieces),)))
    else:
        in_specs += [whole_block(right), pl.BlockSpec(memory_space=pl.ANY)]
    flops = 2 * steps * ROWS * lanes * 1024
    return pl.pallas_call(
        functools.partial(enlarge_kernel, layout_of(pieces) if pieces else ()),
        grid=(steps,),
        in_specs=in_specs,
        out_specs=out_specs,
        out_shape=out_shape,
        scratch_shapes=scratch,
        compiler_params=pltpu.CompilerParams(dimension_semantics=("arbitrary",), vmem_limit_bytes=60 << 20),
        cost_estimate=pl.CostEstimate(flops=flops, transcendentals=0, bytes_accessed=steps * out_rows * lanes * 2),
        input_output_aliases={} if pieces else {len(in_specs) - 1: 0},
        name="enlarge",
    )(order, half_left, first, second, *([p for _, _, p in pieces] if pieces else [right, before]))


def project_kernel(layout, order_ref, spot_ref, rows_ref, *refs):
    count = len(layout)
    if count:
        pieces, (out_ref, basis_all, stage, sems) = refs[:count], refs[count:]

        @pl.when(pl.program_id(0) == 0)
        def _():
            assemble(layout, order_ref, pieces, stage, basis_all, sems)
    else:
        basis_all, out_ref = refs
    out_ref[...] = lax.dot_general(rows_ref[...], basis_all[...], (((1,), (1,)), ((), ())),
                                   preferred_element_type=F32).astype(out_ref.dtype)


def project(enlarged, basis, order, spot, rows, width):
    lanes = enlarged.shape[1]
    pieces = basis if isinstance(basis, list) else None
    once = rows // SPLIT
    full = lambda shape: pl.BlockSpec(shape, lambda s, order, spot: (0,) * len(shape), pipeline_mode=pl.Buffered(1))
    in_specs = [pl.BlockSpec((once, lanes), lambda s, order, spot: (spot[0] * SPLIT + s, 0))]
    out_specs = [pl.BlockSpec((once, width), lambda s, order, spot: (s, 0))]
    out_shape = [jax.ShapeDtypeStruct((rows, width), BF16)]
    scratch = []
    if pieces:
        in_specs += [pl.BlockSpec(memory_space=pl.ANY)] * len(pieces)
        out_specs.append(full((width, lanes)))
        out_shape.append(jax.ShapeDtypeStruct((width, lanes), BF16))
        scratch += [pltpu.VMEM(shape_of(pieces), BF16), pltpu.SemaphoreType.DMA((len(pieces),))]
    else:
        in_specs.append(full(basis.shape))
    return pl.pallas_call(
        functools.partial(project_kernel, layout_of(pieces) if pieces else ()),
        grid_spec=pltpu.PrefetchScalarGridSpec(
            num_scalar_prefetch=2, grid=(SPLIT,), in_specs=in_specs, out_specs=out_specs, scratch_shapes=scratch),
        out_shape=out_shape,
        compiler_params=pltpu.CompilerParams(dimension_semantics=("arbitrary",), vmem_limit_bytes=60 << 20),
        cost_estimate=pl.CostEstimate(flops=2 * rows * width * lanes, transcendentals=0,
                                      bytes_accessed=2 * rows * lanes),
        name="project",
    )(order, spot, enlarged, *([p for _, _, p in pieces] if pieces else [basis]))


def factor_kernel(real, gram_ref, upper_ref, inverse_ref, work, cell):
    blocks = work.shape[0]
    size = blocks * BLOCK
    lane = lax.broadcasted_iota(jnp.int32, (BLOCK, size), 1)
    row = lax.broadcasted_iota(jnp.int32, (BLOCK, size), 0)
    place = 0
    for k in range(blocks):
        unit = (lane == row + k * BLOCK).astype(F32)
        work[k, :, :size] = jnp.where(lane >= real, unit, 0.0)
        work[k, :, size:] = unit
        for j in range(k, blocks):
            at = slice(j * BLOCK, (j + 1) * BLOCK)
            work[k, :, at] = work[k, :, at] + gram_ref[place * BLOCK:(place + 1) * BLOCK, :]
            place += 1
    sub = lax.broadcasted_iota(jnp.int32, (PANEL, BLOCK), 0)
    lane8 = lax.broadcasted_iota(jnp.int32, (PANEL, BLOCK), 1)
    panels = BLOCK // PANEL

    def block_step(k, carry):
        here = pl.ds(pl.multiple_of(k * BLOCK, BLOCK), BLOCK)
        cell[:, :BLOCK] = work[k, :, here]
        row_b = lax.broadcasted_iota(jnp.int32, (BLOCK, BLOCK), 0)
        lane_b = lax.broadcasted_iota(jnp.int32, (BLOCK, BLOCK), 1)
        cell[:, BLOCK:] = (row_b == lane_b).astype(F32)
        for p in range(panels):
            base = p * PANEL
            left = cell[base:base + PANEL, :BLOCK]
            right = cell[base:base + PANEL, BLOCK:]
            spread = [jnp.broadcast_to(left[:, base + t:base + t + 1], (PANEL, BLOCK)) for t in range(PANEL)]
            scale = jnp.zeros((PANEL, BLOCK), F32)
            for t in range(PANEL):
                inv = 1.0 / jnp.broadcast_to(spread[t][t:t + 1, :], (PANEL, BLOCK))
                factor = jnp.where(sub > t, spread[t] * inv, 0.0)
                scale = jnp.where(sub == t, inv, scale)
                for later in range(t + 1, PANEL):
                    spread[later] = spread[later] - factor * jnp.broadcast_to(
                        spread[later][t:t + 1, :], (PANEL, BLOCK))
                left = left - factor * jnp.broadcast_to(left[t:t + 1, :], (PANEL, BLOCK))
                right = right - factor * jnp.broadcast_to(right[t:t + 1, :], (PANEL, BLOCK))
            weights = jnp.transpose(left * scale)
            for g in range(p + 1, panels):
                at = slice(g * PANEL, (g + 1) * PANEL)
                a, b = cell[at, :BLOCK], cell[at, BLOCK:]
                for t in range(PANEL):
                    w = jnp.broadcast_to(weights[at, t:t + 1], (PANEL, BLOCK))
                    a = a - w * jnp.broadcast_to(left[t:t + 1, :], (PANEL, BLOCK))
                    b = b - w * jnp.broadcast_to(right[t:t + 1, :], (PANEL, BLOCK))
                cell[at, :BLOCK] = a
                cell[at, BLOCK:] = b
            root = jnp.sqrt(scale)
            cell[base:base + PANEL, BLOCK:] = right * root
        low = cell[:, BLOCK:]
        mine = jnp.dot(low, work[k], precision=HIGHEST, preferred_element_type=F32)
        work[k] = mine

        def update(i, c):
            there = pl.ds(pl.multiple_of(i * BLOCK, BLOCK), BLOCK)
            work[i] = work[i] - lax.dot_general(work[k, :, there], mine, (((0,), (0,)), ((), ())),
                                                precision=HIGHEST, preferred_element_type=F32)
            return c

        lax.fori_loop(k + 1, blocks, update, 0)
        return carry

    lax.fori_loop(0, blocks, block_step, 0)
    for k in range(blocks):
        count = min(BLOCK, real - k * BLOCK)
        at = slice(k * BLOCK, k * BLOCK + count)
        upper = jnp.where(lane >= row + k * BLOCK, work[k, :, :size], 0.0)
        upper_ref[at, :] = upper[:count, :real]
        inverse_ref[at, :] = work[k, :count, size:size + real]


def packed_blocks(gram):
    real = gram.shape[0]
    spare = -real % BLOCK
    gram = jnp.pad(gram, ((0, spare), (0, spare)))
    blocks = gram.shape[0] // BLOCK
    return jnp.concatenate([gram[i * BLOCK:(i + 1) * BLOCK, j * BLOCK:(j + 1) * BLOCK]
                            for i in range(blocks) for j in range(i, blocks)])


def factorize(packed, real):
    blocks = -(-real // BLOCK)
    size = blocks * BLOCK
    return pl.pallas_call(
        functools.partial(factor_kernel, real),
        out_shape=(jax.ShapeDtypeStruct((real, real), F32),) * 2,
        scratch_shapes=[pltpu.VMEM((blocks, BLOCK, 2 * size), F32), pltpu.VMEM((BLOCK, 2 * BLOCK), F32)],
        compiler_params=pltpu.CompilerParams(vmem_limit_bytes=60 << 20),
        name="factor",
    )(packed)


def solve_kernel(count, spots_ref, own_ref, inverse_ref, *refs):
    pieces, (out_ref, stage, value, sems) = refs[:count], refs[count:]
    copies = [pltpu.make_async_copy(piece, stage.at[spots_ref[s]], sems.at[s]) for s, piece in enumerate(pieces)]
    for copy in copies:
        copy.start()
    _, outer, cols = out_ref.shape
    low = inverse_ref[pl.ds(pl.multiple_of(own_ref[0] * cols, 8), cols), :]
    terms = []
    for _ in range(3):
        term = low.astype(BF16)
        low = low - term.astype(F32)
        terms.append(term)
    for copy in copies:
        copy.wait()
    rows = stage.shape[1]

    def one_part(n, carry):
        data = stage[n]
        value[pl.ds(pl.multiple_of(n * rows, 8), rows), :] = sum(
            lax.dot_general(data, term, (((1,), (1,)), ((), ())), preferred_element_type=F32) for term in terms)
        return carry

    lax.fori_loop(0, count, one_part, 0)
    pairs = outer // 2
    for d in range(BOND):
        for e in range(BOND):
            for i in range(2):
                data = value[pl.ds(d * 16 + i * 8 + e, pairs, stride=BOND * 16), :]
                out_ref[d * BOND + e, pl.ds(i, pairs, stride=2), :] = data


def solve(pieces, inverse, spots, own, cols):
    rows, width = pieces[0].shape
    outer = rows * len(pieces) // (BOND * 8)
    smem = pl.BlockSpec(memory_space=pltpu.SMEM)
    return pl.pallas_call(
        functools.partial(solve_kernel, len(pieces)),
        in_specs=[smem, smem, pl.BlockSpec(memory_space=pltpu.VMEM)] + [pl.BlockSpec(memory_space=pl.ANY)] * len(pieces),
        out_shape=jax.ShapeDtypeStruct((BOND * BOND, outer, cols), F32),
        scratch_shapes=[pltpu.VMEM((len(pieces), rows, width), BF16), pltpu.VMEM((rows * len(pieces), cols), F32),
                        pltpu.SemaphoreType.DMA((len(pieces),))],
        compiler_params=pltpu.CompilerParams(vmem_limit_bytes=60 << 20),
        name="solve",
    )(spots, own, inverse, *pieces)


def swap(x, mask):
    count = lax.axis_size("wide") * lax.axis_size("narrow")
    return lax.ppermute(x, ("wide", "narrow"), [(i, i ^ mask) for i in range(count)])


def bits_of(axis):
    return lax.axis_size(axis).bit_length() - 1


def gather_wide(x, after=()):
    if after:
        x = lax.optimization_barrier((x,) + tuple(after))[0]
    if lax.axis_size("wide") != 8:
        whole = lax.all_gather(x, "wide", axis=1, tiled=True)
        return [(0, 0, whole)], [whole]
    low = lax.axis_size("narrow")
    one, two, six = low, 2 * low, 6 * low
    blocks = {0: x, 1: swap(x, one), 2: swap(x, two), 6: swap(x, six)}
    blocks[3] = swap(blocks[2], one)
    blocks[4] = swap(blocks[6], two)
    blocks[7] = swap(blocks[1], six)
    blocks[5] = swap(blocks[4], one)
    return [(m, 0, blocks[m]) for m in range(8)], [blocks[3], blocks[5], blocks[7]]


def gather_narrow(x):
    blocks = [x]
    for bit in reversed(range(bits_of("narrow"))):
        blocks = blocks + [swap(b, 1 << bit) for b in blocks]
    return blocks


def narrow_masks():
    masks = [0]
    for bit in reversed(range(bits_of("narrow"))):
        masks = masks + [m | (1 << bit) for m in masks]
    return masks


def groups():
    bits = bits_of("narrow") + bits_of("wide")
    first = bits % 2
    out = [[1]] if first else []
    for b in range(first, bits, 2):
        out.append([1 << b, 2 << b])
    return out


def place_in(group, me):
    place, masks = 0, [0]
    for n, mask in enumerate(group):
        place = place + (((me // mask) % 2) << n)
        masks = masks + [m | mask for m in masks]
    return place, masks


def sum_group(x, group, me):
    place, masks = place_in(group, me)
    parts = x.reshape(len(masks), x.shape[0] // len(masks), x.shape[1])
    total = lax.dynamic_index_in_dim(parts, place, 0, False)
    for n, mask in list(enumerate(masks))[1:]:
        total = total + swap(lax.dynamic_index_in_dim(parts, place ^ n, 0, False), mask)
    return total


def join_group(x, group, me):
    place, masks = place_in(group, me)
    parts = jnp.stack([x] + [swap(x, mask) for mask in masks[1:]])
    return jnp.concatenate([lax.dynamic_index_in_dim(parts, place ^ n, 0, False) for n in range(len(masks))])


def move(left_edge, corner, right_edge, single_layer, warm_basis):
    local_rows, square, depth = left_edge.shape
    breadth = corner.shape[1]
    local_cols = right_edge.shape[2]
    narrow = lax.axis_size("narrow")
    own = lax.axis_index("narrow").astype(jnp.int32)
    me = lax.axis_index("wide").astype(jnp.int32) * narrow + own

    right, ahead = gather_wide(right_edge.transpose(1, 0, 2))
    lefts = [x.reshape(square * local_rows, depth) for x in gather_narrow(left_edge.transpose(1, 0, 2))]
    corners = gather_narrow(corner)
    half_left = half_left_of(lefts, corners, local_rows + -local_rows % OUTER)
    first, second = site_operands(single_layer)
    order = jnp.arange(shape_of(right)[0], dtype=jnp.int32)
    if len(right) > 1:
        order = order ^ (me // narrow)
    basis, _ = gather_wide(warm_basis.transpose(0, 2, 1), ahead)

    steps = half_left.shape[0] // ROWS
    cuts = [0, 3, 5, steps] if steps > 5 else [0, steps]
    enlarged = None
    for n in range(len(cuts) - 1):
        made = enlarge(half_left, right, order, first, second, cuts[n], cuts[n + 1] - cuts[n], enlarged)
        enlarged = made[0]
        if n == 0:
            right = made[1]

    half = enlarged.shape[0] // 2
    spot = lambda *masks: jnp.stack([own ^ m for m in masks])

    def summed(product):
        parts = product.reshape(2, half // 2, breadth)
        mine = lax.dynamic_index_in_dim(parts, own % 2, 0, False)
        other = swap(lax.dynamic_index_in_dim(parts, 1 - own % 2, 0, False), 1)
        return mine.astype(F32) + other.astype(F32)

    product, basis = project(enlarged, basis, order, (1 - own // 2)[None], half, breadth)
    near = summed(product).astype(BF16)
    enlarged, near = lax.optimization_barrier((enlarged, near))
    near = swap(near, 2)
    product = project(enlarged, basis, order, (own // 2)[None], half, breadth)
    rows = (summed(product[0]) + near.astype(F32)).astype(BF16)

    gram = lax.dot_general(rows, rows, (((0,), (0,)), ((), ())), preferred_element_type=F32) / (breadth * square)
    gram = packed_blocks(gram)
    for group in groups():
        gram = sum_group(gram, group, me)
    for group in reversed(groups()):
        gram = join_group(gram, group, me)
    rows, gram = lax.optimization_barrier((rows, gram))
    pieces = gather_narrow(rows)
    upper, inverse = factorize(gram, breadth)
    new_basis = solve(pieces, inverse, spot(*narrow_masks()), own[None], local_cols)
    return new_basis.transpose(1, 0, 2)[:local_rows], upper


def solution(mesh):
    placed = (
        P("wide", None, "narrow"),
        P("narrow", None),
        P("wide", None, "narrow"),
        P(),
        P(None, "narrow", "wide"),
    )
    return jax.shard_map(
        move,
        mesh=mesh,
        in_specs=placed,
        out_specs=(P("wide", None, "narrow"), P()),
        check_vma=False,
    )
```

profile of v0, /device:TPU:0, one launch (start us, length us, event | category | flops | bytes accessed | tf_op | source)
XLA Modules:
  0.0 347.3 jit_solution(10366412839462227688)
XLA Ops:
  0.6 5.1 %collective-permute-start.9 = (bf16[49,56,112]{2,1,0:T(8,128)(2,1)}, bf16[49,56,112]{2,1,0:T(8,128)(2,1)S(1)}, u32[]{:S(2)}, u32[]{:S(2)}) collective-permute-start(bf16[49,56,112]{2,1,0:T(8,128)(2,1)} %bitcast.126), channel_id=1, source_target_pairs={{0,24},{1,25},{2,26},{3,27},{4,28},{5,29},{6,30},{7,31},{8,16},{9,... | collective-permute-start | bytes 1843976 | tf_op jit(solution)/shard_map/ppermute | solution.py:379
  8.8 13.9 %collective-permute-done.9.rest_6_ = bf16[49,56,112]{2,1,0:T(8,128)(2,1)S(1)} collective-permute-done((bf16[49,56,112]{2,1,0:T(8,128)(2,1)}, bf16[49,56,112]{2,1,0:T(8,128)(2,1)S(1)}, u32[]{:S(2)}, u32[]{:S(2)}) %collective-permute-start.9) | collective-permute-done | bytes 614688 | tf_op jit(solution)/shard_map/ppermute | solution.py:379
  22.7 13.8 %collective-permute-start.10 = (bf16[49,56,112]{2,1,0:T(8,128)(2,1)S(1)}, bf16[49,56,112]{2,1,0:T(8,128)(2,1)}, u32[]{:S(2)}, u32[]{:S(2)}) collective-permute-start(bf16[49,56,112]{2,1,0:T(8,128)(2,1)S(1)} %collective-permute-done.9.rest_6_), channel_id=1, source_target_pairs={{0,8},{1,9},{2,10},{3,11},{4,12},{5,13},{6,14},{7,15},{8,0},{9,1},... | collective-permute-start | bytes 1843976 | tf_op jit(solution)/shard_map/ppermute | solution.py:379
  38.0 3.5 %collective-permute-done.3.refs_5_ = bf16[112,448]{1,0:T(8,128)(2,1)S(1)} collective-permute-done((bf16[112,448]{1,0:T(8,128)(2,1)}, bf16[112,448]{1,0:T(8,128)(2,1)S(1)}, u32[]{:S(2)}, u32[]{:S(2)}) %collective-permute-start.3) | collective-permute-done | bytes 100384 | tf_op jit(solution)/shard_map/ppermute | solution.py:379
  44.9 2.5 collective-permute-start.12
  48.9 3.7 %collective-permute-done.10.rest_4_ = bf16[49,56,112]{2,1,0:T(8,128)(2,1)} collective-permute-done((bf16[49,56,112]{2,1,0:T(8,128)(2,1)S(1)}, bf16[49,56,112]{2,1,0:T(8,128)(2,1)}, u32[]{:S(2)}, u32[]{:S(2)}) %collective-permute-start.10) | collective-permute-done | bytes 614688 | tf_op jit(solution)/shard_map/ppermute | solution.py:379
  56.3 2.2 mul.24.first_ref
  60.9 14.0 %half_left.1.half_ref = bf16[3584,448]{1,0:T(8,128)(2,1)} custom-call(bf16[2744,112]{1,0:T(8,128)(2,1)} %bitcast.115, bf16[2744,112]{1,0:T(8,128)(2,1)} %bitcast.7.refs_1_, bf16[2744,112]{1,0:T(8,128)(2,1)} %bitcast.8.refs_2_, bf16[2744,112]{1,0:T(8,128)(2,1)} %bitcast.9.refs_3_, bf16[112,448]{1,0:T(8,128)(2,1)} %refs_4_.1, bf16[112,448]{1,0:T(8,128)(2,1)} %copy-done.13, ...), custom_call_target="tpu_custom_call" | custom-call | tf_op jit(solution)/shard_map/half_left/pallas_call | solution.py:89
  74.8 5.5 %collective-permute-done.11.rest_5_ = bf16[49,56,112]{2,1,0:T(8,128)(2,1)} collective-permute-done((bf16[49,56,112]{2,1,0:T(8,128)(2,1)}, bf16[49,56,112]{2,1,0:T(8,128)(2,1)}, u32[]{:S(2)}, u32[]{:S(2)}) %collective-permute-start.11) | collective-permute-done | bytes 614688 | tf_op jit(solution)/shard_map/ppermute | solution.py:379
  83.2 39.2 %enlarge.3 = (bf16[3136,6272]{1,0:T(8,128)(2,1)}, bf16[448,6272]{1,0:T(8,128)(2,1)}) custom-call(s32[8]{0:T(128)} %iota_xor_fusion.order_ref, bf16[3584,448]{1,0:T(8,128)(2,1)} %half_left.1.half_ref, bf16[392,224]{1,0:T(8,128)(2,1)} %mul.24.first_ref, bf16[56,112]{1,0:T(8,128)(2,1)} %copy.15.second_ref, bf16[49,56,112]{2,1,0:T(8,128)(2,1)} %bitcast.129, ...), custom_call_target="tpu_custom_call" | custom-call | flops 19730006016 | bytes 16859136 | tf_op jit(solution)/shard_map/enlarge/pallas_call | solution.py:181
  122.4 2.1 collective-permute-start.17
  124.5 25.1 %enlarge.4.rest_1_ = bf16[3136,6272]{1,0:T(8,128)(2,1)} custom-call(s32[8]{0:T(128)} %iota_xor_fusion.order_ref, bf16[3584,448]{1,0:T(8,128)(2,1)} %half_left.1.half_ref, bf16[392,224]{1,0:T(8,128)(2,1)} %mul.24.first_ref, bf16[56,112]{1,0:T(8,128)(2,1)} %copy.15.second_ref, ...), custom_call_target="tpu_custom_call", output_to_operand_aliasing={{}: (5, {})} | custom-call | flops 13153337344 | bytes 11239424 | tf_op jit(solution)/shard_map/enlarge/pallas_call | solution.py:181
  150.2 2.5 collective-permute-start.19
  154.3 25.1 %enlarge.5.rows_ref = bf16[3136,6272]{1,0:T(8,128)(2,1)} custom-call(s32[8]{0:T(128)} %iota_xor_fusion.order_ref, bf16[3584,448]{1,0:T(8,128)(2,1)} %half_left.1.half_ref, bf16[392,224]{1,0:T(8,128)(2,1)} %mul.24.first_ref, bf16[56,112]{1,0:T(8,128)(2,1)} %copy.15.second_ref, ...), custom_call_target="tpu_custom_call", output_to_operand_aliasing={{}: (5, {})} | custom-call | flops 13153337344 | bytes 11239424 | tf_op jit(solution)/shard_map/enlarge/pallas_call | solution.py:181
  181.3 21.9 %project.2 = (bf16[1568,448]{1,0:T(8,128)(2,1)}, bf16[448,6272]{1,0:T(8,128)(2,1)}) custom-call(s32[8]{0:T(128)} %iota_xor_fusion.order_ref, s32[1]{0:T(128)} %bitcast.14.spot_ref, bf16[3136,6272]{1,0:T(8,128)(2,1)} %enlarge.5.rows_ref, bf16[49,56,112]{2,1,0:T(8,128)(2,1)} %bitcast.109, bf16[49,56,112]{2,1,0:T(8,128)(2,1)} %copy-done.9, ...), custom_call_target="tpu_custom_call" | custom-call | flops 8811708416 | bytes 19668992 | tf_op jit(solution)/shard_map/project/pallas_call | solution.py:225
  204.6 2.3 collective-permute-done.20
  207.1 17.7 %project.3 = bf16[1568,448]{1,0:T(8,128)(2,1)} custom-call(s32[8]{0:T(128)} %iota_xor_fusion.order_ref, s32[1]{0:T(128)} %bitcast.4.spot_ref, bf16[3136,6272]{1,0:T(8,128)(2,1)} %enlarge.5.rows_ref, bf16[448,6272]{1,0:T(8,128)(2,1)} %get-tuple-element.18.refs_0_), custom_call_target="tpu_custom_call" | custom-call | flops 8811708416 | bytes 19668992 | tf_op jit(solution)/shard_map/project/pallas_call | solution.py:225
  224.8 2.2 dynamic-slice_bitcast_fusion
  229.5 17.9 %collective-permute-done.22 = bf16[784,448]{1,0:T(8,128)(2,1)} collective-permute-done((bf16[784,448]{1,0:T(8,128)(2,1)S(1)}, bf16[784,448]{1,0:T(8,128)(2,1)}, u32[]{:S(2)}, u32[]{:S(2)}) %collective-permute-start.22) | collective-permute-done | bytes 702496 | tf_op jit(solution)/shard_map/ppermute | solution.py:379
  256.1 3.2 collective-permute-done.25
  259.4 1.6 collective-permute-start.27
  263.8 2.0 collective-permute-done.28
  265.8 2.3 collective-permute-done.29
  268.1 1.9 collective-permute-start.31
  270.0 2.5 collective-permute-start.32
  272.9 2.7 collective-permute-done.32
  277.5 1.7 collective-permute-start.35
  280.7 2.2 collective-permute-done.35
  283.1 1.6 collective-permute-done.36
  287.1 18.5 %collective-permute-done.37.refs_1_ = bf16[784,448]{1,0:T(8,128)(2,1)S(1)} collective-permute-done((bf16[784,448]{1,0:T(8,128)(2,1)S(1)}, bf16[784,448]{1,0:T(8,128)(2,1)S(1)}, u32[]{:S(2)}, u32[]{:S(2)}) %collective-permute-start.37) | collective-permute-done | bytes 702496 | tf_op jit(solution)/shard_map/ppermute | solution.py:379
  306.3 31.9 %factor.1 = (f32[448,448]{1,0:T(8,128)}, f32[448,448]{1,0:T(8,128)}) custom-call(f32[1280,128]{1,0:T(8,128)} %pad_maximum_fusion.gram_ref), custom_call_target="tpu_custom_call" | custom-call | tf_op jit(solution)/shard_map/factor/pallas_call | solution.py:322
  339.4 7.8 %solve.1 = f32[49,56,112]{2,1,0:T(8,128)} custom-call(s32[4]{0:T(128)} %pad_add_fusion.spots_ref, s32[1]{0:T(128)} %bitcast.own_ref, f32[448,448]{1,0:T(8,128)} %get-tuple-element.21.inverse_ref, bf16[784,448]{1,0:T(8,128)(2,1)} %copy-done.1, bf16[784,448]{1,0:T(8,128)(2,1)} %copy-done.3, bf16[784,448]{1,0:T(8,128)(2,1)} %copy-done.4, bf16[784,448]{1,0:T(8,128)(2,1)} %copy-done.5), custom_call_target="tpu_custom_call" | custom-call | tf_op jit(solution)/shard_map/solve/pallas_call | solution.py:366
  (132 shorter events, 46.1 us)
Async XLA Ops:
  0.6 22.0 %collective-permute-start.9 = (bf16[49,56,112]{2,1,0:T(8,128)(2,1)}, bf16[49,56,112]{2,1,0:T(8,128)(2,1)S(1)}, u32[]{:S(2)}, u32[]{:S(2)}) collective-permute-start(bf16[49,56,112]{2,1,0:T(8,128)(2,1)} %bitcast.126), channel_id=1, source_target_pairs={{0,24},{1,25},{2,26},{3,27},{4,28},{5,29},{6,30},{7,31},{8,16},{9,... | collective-permute-start | bytes 1843976 | tf_op jit(solution)/shard_map/ppermute | solution.py:379
  5.8 38.9 %collective-permute-start = (bf16[49,56,112]{2,1,0:T(8,128)(2,1)}, bf16[49,56,112]{2,1,0:T(8,128)(2,1)}, u32[]{:S(2)}, u32[]{:S(2)}) collective-permute-start(bf16[49,56,112]{2,1,0:T(8,128)(2,1)} %bitcast.113), channel_id=1, source_target_pairs={{0,2},{1,3},{2,0},{3,1},{4,6},{5,7},{6,4},{7,5},{8,10},{9,11},{10,... | collective-permute-start | bytes 1843976 | tf_op jit(solution)/shard_map/ppermute | solution.py:379
  7.3 37.6 %collective-permute-start.6 = (bf16[49,56,112]{2,1,0:T(8,128)(2,1)}, bf16[49,56,112]{2,1,0:T(8,128)(2,1)}, u32[]{:S(2)}, u32[]{:S(2)}) collective-permute-start(bf16[49,56,112]{2,1,0:T(8,128)(2,1)} %bitcast.127), channel_id=1, source_target_pairs={{0,4},{1,5},{2,6},{3,7},{4,0},{5,1},{6,2},{7,3},{8,12},{9,13},{10,... | collective-permute-start | bytes 1843976 | tf_op jit(solution)/shard_map/ppermute | solution.py:379
  8.8 38.6 %collective-permute-start.7 = (bf16[49,56,112]{2,1,0:T(8,128)(2,1)}, bf16[49,56,112]{2,1,0:T(8,128)(2,1)}, u32[]{:S(2)}, u32[]{:S(2)}) collective-permute-start(bf16[49,56,112]{2,1,0:T(8,128)(2,1)} %bitcast.128), channel_id=1, source_target_pairs={{0,8},{1,9},{2,10},{3,11},{4,12},{5,13},{6,14},{7,15},{8,0},{9,1},... | collective-permute-start | bytes 1843976 | tf_op jit(solution)/shard_map/ppermute | solution.py:379
  22.7 30.0 %collective-permute-start.10 = (bf16[49,56,112]{2,1,0:T(8,128)(2,1)S(1)}, bf16[49,56,112]{2,1,0:T(8,128)(2,1)}, u32[]{:S(2)}, u32[]{:S(2)}) collective-permute-start(bf16[49,56,112]{2,1,0:T(8,128)(2,1)S(1)} %collective-permute-done.9.rest_6_), channel_id=1, source_target_pairs={{0,8},{1,9},{2,10},{3,11},{4,12},{5,13},{6,14},{7,15},{8,0},{9,1},... | collective-permute-start | bytes 1843976 | tf_op jit(solution)/shard_map/ppermute | solution.py:379
  36.5 5.0 %collective-permute-start.3 = (bf16[112,448]{1,0:T(8,128)(2,1)}, bf16[112,448]{1,0:T(8,128)(2,1)S(1)}, u32[]{:S(2)}, u32[]{:S(2)}) collective-permute-start(bf16[112,448]{1,0:T(8,128)(2,1)} %refs_4_.1), channel_id=1, source_target_pairs={{0,2},{1,3},{2,0},{3,1},{4,6},{5,7},{6,4},{7,5},{8,10},{9,11},{10,... | collective-permute-start | bytes 301064 | tf_op jit(solution)/shard_map/ppermute | solution.py:379
  44.4 16.5 %collective-permute-start.1 = (bf16[49,56,112]{2,1,0:T(8,128)(2,1)}, bf16[49,56,112]{2,1,0:T(8,128)(2,1)}, u32[]{:S(2)}, u32[]{:S(2)}) collective-permute-start(bf16[49,56,112]{2,1,0:T(8,128)(2,1)} %bitcast.114), channel_id=1, source_target_pairs={{0,1},{1,0},{2,3},{3,2},{4,5},{5,4},{6,7},{7,6},{8,9},{9,8},{10,11... | collective-permute-start | bytes 1843976 | tf_op jit(solution)/shard_map/ppermute | solution.py:379
  44.6 16.2 %collective-permute-start.2 = (bf16[49,56,112]{2,1,0:T(8,128)(2,1)}, bf16[49,56,112]{2,1,0:T(8,128)(2,1)}, u32[]{:S(2)}, u32[]{:S(2)}) collective-permute-start(bf16[49,56,112]{2,1,0:T(8,128)(2,1)} %collective-permute-done), channel_id=1, source_target_pairs={{0,1},{1,0},{2,3},{3,2},{4,5},{5,4},{6,7},{7,6},{8,9},{9,8},{10,11... | collective-permute-start | bytes 1843976 | tf_op jit(solution)/shard_map/ppermute | solution.py:379
  44.9 30.0 %collective-permute-start.12 = (bf16[49,56,112]{2,1,0:T(8,128)(2,1)}, bf16[49,56,112]{2,1,0:T(8,128)(2,1)}, u32[]{:S(2)}, u32[]{:S(2)}) collective-permute-start(bf16[49,56,112]{2,1,0:T(8,128)(2,1)} %collective-permute-done.6.rest_1_), channel_id=1, source_target_pairs={{0,24},{1,25},{2,26},{3,27},{4,28},{5,29},{6,30},{7,31},{8,16},{9,... | collective-permute-start | bytes 1843976 | tf_op jit(solution)/shard_map/ppermute | solution.py:379
  47.4 27.5 %collective-permute-start.8 = (bf16[49,56,112]{2,1,0:T(8,128)(2,1)}, bf16[49,56,112]{2,1,0:T(8,128)(2,1)}, u32[]{:S(2)}, u32[]{:S(2)}) collective-permute-start(bf16[49,56,112]{2,1,0:T(8,128)(2,1)} %collective-permute-done.7.rest_2_), channel_id=1, source_target_pairs={{0,4},{1,5},{2,6},{3,7},{4,0},{5,1},{6,2},{7,3},{8,12},{9,13},{10,... | collective-permute-start | bytes 1843976 | tf_op jit(solution)/shard_map/ppermute | solution.py:379
  52.6 27.7 %collective-permute-start.11 = (bf16[49,56,112]{2,1,0:T(8,128)(2,1)}, bf16[49,56,112]{2,1,0:T(8,128)(2,1)}, u32[]{:S(2)}, u32[]{:S(2)}) collective-permute-start(bf16[49,56,112]{2,1,0:T(8,128)(2,1)} %collective-permute-done.10.rest_4_), channel_id=1, source_target_pairs={{0,4},{1,5},{2,6},{3,7},{4,0},{5,1},{6,2},{7,3},{8,12},{9,13},{10,... | collective-permute-start | bytes 1843976 | tf_op jit(solution)/shard_map/ppermute | solution.py:379
  80.4 42.1 %collective-permute-start.16 = (bf16[49,56,112]{2,1,0:T(8,128)(2,1)S(1)}, bf16[49,56,112]{2,1,0:T(8,128)(2,1)S(1)}, u32[]{:S(2)}, u32[]{:S(2)}) collective-permute-start(bf16[49,56,112]{2,1,0:T(8,128)(2,1)S(1)} %bitcast.110), channel_id=1, source_target_pairs={{0,24},{1,25},{2,26},{3,27},{4,28},{5,29},{6,30},{7,31},{8,16},{9,... | collective-permute-start | bytes 1843976 | tf_op jit(solution)/shard_map/ppermute | solution.py:379
  81.7 68.0 %collective-permute-start.14 = (bf16[49,56,112]{2,1,0:T(8,128)(2,1)S(1)}, bf16[49,56,112]{2,1,0:T(8,128)(2,1)S(1)}, u32[]{:S(2)}, u32[]{:S(2)}) collective-permute-start(bf16[49,56,112]{2,1,0:T(8,128)(2,1)S(1)} %bitcast.111), channel_id=1, source_target_pairs={{0,8},{1,9},{2,10},{3,11},{4,12},{5,13},{6,14},{7,15},{8,0},{9,1},... | collective-permute-start | bytes 1843976 | tf_op jit(solution)/shard_map/ppermute | solution.py:379
  81.7 68.5 %collective-permute-start.13 = (bf16[49,56,112]{2,1,0:T(8,128)(2,1)S(1)}, bf16[49,56,112]{2,1,0:T(8,128)(2,1)S(1)}, u32[]{:S(2)}, u32[]{:S(2)}) collective-permute-start(bf16[49,56,112]{2,1,0:T(8,128)(2,1)S(1)} %bitcast.112), channel_id=1, source_target_pairs={{0,4},{1,5},{2,6},{3,7},{4,0},{5,1},{6,2},{7,3},{8,12},{9,13},{10,... | collective-permute-start | bytes 1843976 | tf_op jit(solution)/shard_map/ppermute | solution.py:379
  122.4 30.3 %collective-permute-start.17 = (bf16[49,56,112]{2,1,0:T(8,128)(2,1)S(1)}, bf16[49,56,112]{2,1,0:T(8,128)(2,1)S(1)}, u32[]{:S(2)}, u32[]{:S(2)}) collective-permute-start(bf16[49,56,112]{2,1,0:T(8,128)(2,1)S(1)} %collective-permute-done.16.refs_6_), channel_id=1, source_target_pairs={{0,8},{1,9},{2,10},{3,11},{4,12},{5,13},{6,14},{7,15},{8,0},{9,1},... | collective-permute-start | bytes 1843976 | tf_op jit(solution)/shard_map/ppermute | solution.py:379
  149.7 29.7 %collective-permute-start.15 = (bf16[49,56,112]{2,1,0:T(8,128)(2,1)S(1)}, bf16[49,56,112]{2,1,0:T(8,128)(2,1)}, u32[]{:S(2)}, u32[]{:S(2)}) collective-permute-start(bf16[49,56,112]{2,1,0:T(8,128)(2,1)S(1)} %collective-permute-done.14.refs_2_), channel_id=1, source_target_pairs={{0,4},{1,5},{2,6},{3,7},{4,0},{5,1},{6,2},{7,3},{8,12},{9,13},{10,... | collective-permute-start | bytes 1843976 | tf_op jit(solution)/shard_map/ppermute | solution.py:379
  150.2 29.1 %collective-permute-start.19 = (bf16[49,56,112]{2,1,0:T(8,128)(2,1)S(1)}, bf16[49,56,112]{2,1,0:T(8,128)(2,1)S(1)}, u32[]{:S(2)}, u32[]{:S(2)}) collective-permute-start(bf16[49,56,112]{2,1,0:T(8,128)(2,1)S(1)} %collective-permute-done.13.refs_1_), channel_id=1, source_target_pairs={{0,24},{1,25},{2,26},{3,27},{4,28},{5,29},{6,30},{7,31},{8,16},{9,... | collective-permute-start | bytes 1843976 | tf_op jit(solution)/shard_map/ppermute | solution.py:379
  152.7 27.7 %collective-permute-start.18 = (bf16[49,56,112]{2,1,0:T(8,128)(2,1)S(1)}, bf16[49,56,112]{2,1,0:T(8,128)(2,1)S(1)}, u32[]{:S(2)}, u32[]{:S(2)}) collective-permute-start(bf16[49,56,112]{2,1,0:T(8,128)(2,1)S(1)} %collective-permute-done.17.refs_4_), channel_id=1, source_target_pairs={{0,4},{1,5},{2,6},{3,7},{4,0},{5,1},{6,2},{7,3},{8,12},{9,13},{10,... | collective-permute-start | bytes 1843976 | tf_op jit(solution)/shard_map/ppermute | solution.py:379
  227.1 20.3 %collective-permute-start.22 = (bf16[784,448]{1,0:T(8,128)(2,1)S(1)}, bf16[784,448]{1,0:T(8,128)(2,1)}, u32[]{:S(2)}, u32[]{:S(2)}) collective-permute-start(bf16[784,448]{1,0:T(8,128)(2,1)S(1)} %fusion.2), channel_id=1, source_target_pairs={{0,2},{1,3},{2,0},{3,1},{4,6},{5,7},{6,4},{7,5},{8,10},{9,11},{10,... | collective-permute-start | bytes 2107400 | tf_op jit(solution)/shard_map/ppermute | solution.py:379
  251.5 4.6 %collective-permute-start.24 = (f32[160,128]{1,0:T(8,128)S(1)}, f32[160,128]{1,0:T(8,128)S(1)}, u32[]{:S(2)}, u32[]{:S(2)}) collective-permute-start(f32[160,128]{1,0:T(8,128)S(1)} %get-tuple-element.32), channel_id=1, source_target_pairs={{0,2},{1,3},{2,0},{3,1},{4,6},{5,7},{6,4},{7,5},{8,10},{9,11},{10,... | collective-permute-start | bytes 245768 | tf_op jit(solution)/shard_map/ppermute | solution.py:379
  253.1 6.2 %collective-permute-start.25 = (f32[160,128]{1,0:T(8,128)S(1)}, f32[160,128]{1,0:T(8,128)S(1)}, u32[]{:S(2)}, u32[]{:S(2)}) collective-permute-start(f32[160,128]{1,0:T(8,128)S(1)} %get-tuple-element.34), channel_id=1, source_target_pairs={{0,4},{1,5},{2,6},{3,7},{4,0},{5,1},{6,2},{7,3},{8,12},{9,13},{10,... | collective-permute-start | bytes 245768 | tf_op jit(solution)/shard_map/ppermute | solution.py:379
  253.6 5.7 %collective-permute-start.26 = (f32[160,128]{1,0:T(8,128)S(1)}, f32[160,128]{1,0:T(8,128)S(1)}, u32[]{:S(2)}, u32[]{:S(2)}) collective-permute-start(f32[160,128]{1,0:T(8,128)S(1)} %get-tuple-element.33), channel_id=1, source_target_pairs={{0,6},{1,7},{2,4},{3,5},{4,2},{5,3},{6,0},{7,1},{8,14},{9,15},{10,... | collective-permute-start | bytes 245768 | tf_op jit(solution)/shard_map/ppermute | solution.py:379
  259.4 4.5 %collective-permute-start.27 = (f32[40,128]{1,0:T(8,128)S(1)}, f32[40,128]{1,0:T(8,128)S(1)}, u32[]{:S(2)}, u32[]{:S(2)}) collective-permute-start(f32[40,128]{1,0:T(8,128)S(1)} %get-tuple-element.41), channel_id=1, source_target_pairs={{0,8},{1,9},{2,10},{3,11},{4,12},{5,13},{6,14},{7,15},{8,0},{9,1},... | collective-permute-start | bytes 61448 | tf_op jit(solution)/shard_map/ppermute | solution.py:379
  261.0 4.8 %collective-permute-start.28 = (f32[40,128]{1,0:T(8,128)S(1)}, f32[40,128]{1,0:T(8,128)S(1)}, u32[]{:S(2)}, u32[]{:S(2)}) collective-permute-start(f32[40,128]{1,0:T(8,128)S(1)} %get-tuple-element.43), channel_id=1, source_target_pairs={{0,16},{1,17},{2,18},{3,19},{4,20},{5,21},{6,22},{7,23},{8,24},{9,... | collective-permute-start | bytes 61448 | tf_op jit(solution)/shard_map/ppermute | solution.py:379
  262.5 5.6 %collective-permute-start.29 = (f32[40,128]{1,0:T(8,128)S(1)}, f32[40,128]{1,0:T(8,128)S(1)}, u32[]{:S(2)}, u32[]{:S(2)}) collective-permute-start(f32[40,128]{1,0:T(8,128)S(1)} %get-tuple-element.42), channel_id=1, source_target_pairs={{0,24},{1,25},{2,26},{3,27},{4,28},{5,29},{6,30},{7,31},{8,16},{9,... | collective-permute-start | bytes 61448 | tf_op jit(solution)/shard_map/ppermute | solution.py:379
  268.1 4.7 %collective-permute-start.31 = (f32[40,128]{1,0:T(8,128)S(1)}, f32[40,128]{1,0:T(8,128)S(1)}, u32[]{:S(2)}, u32[]{:S(2)}) collective-permute-start(f32[40,128]{1,0:T(8,128)S(1)} %fusion.13), channel_id=1, source_target_pairs={{0,16},{1,17},{2,18},{3,19},{4,20},{5,21},{6,22},{7,23},{8,24},{9,... | collective-permute-start | bytes 61448 | tf_op jit(solution)/shard_map/ppermute | solution.py:379
  270.0 5.6 %collective-permute-start.32 = (f32[40,128]{1,0:T(8,128)S(1)}, f32[40,128]{1,0:T(8,128)S(1)}, u32[]{:S(2)}, u32[]{:S(2)}) collective-permute-start(f32[40,128]{1,0:T(8,128)S(1)} %fusion.13), channel_id=1, source_target_pairs={{0,24},{1,25},{2,26},{3,27},{4,28},{5,29},{6,30},{7,31},{8,16},{9,... | collective-permute-start | bytes 61448 | tf_op jit(solution)/shard_map/ppermute | solution.py:379
  275.7 4.5 %collective-permute-start.33 = (f32[160,128]{1,0:T(8,128)S(1)}, f32[160,128]{1,0:T(8,128)S(1)}, u32[]{:S(2)}, u32[]{:S(2)}) collective-permute-start(f32[160,128]{1,0:T(8,128)S(1)} %get-tuple-element.36), channel_id=1, source_target_pairs={{0,2},{1,3},{2,0},{3,1},{4,6},{5,7},{6,4},{7,5},{8,10},{9,11},{10,... | collective-permute-start | bytes 245768 | tf_op jit(solution)/shard_map/ppermute | solution.py:379
  277.5 5.3 %collective-permute-start.35 = (f32[160,128]{1,0:T(8,128)S(1)}, f32[160,128]{1,0:T(8,128)S(1)}, u32[]{:S(2)}, u32[]{:S(2)}) collective-permute-start(f32[160,128]{1,0:T(8,128)S(1)} %get-tuple-element.36), channel_id=1, source_target_pairs={{0,6},{1,7},{2,4},{3,5},{4,2},{5,3},{6,0},{7,1},{8,14},{9,15},{10,... | collective-permute-start | bytes 245768 | tf_op jit(solution)/shard_map/ppermute | solution.py:379
  285.7 19.9 %collective-permute-start.37 = (bf16[784,448]{1,0:T(8,128)(2,1)S(1)}, bf16[784,448]{1,0:T(8,128)(2,1)S(1)}, u32[]{:S(2)}, u32[]{:S(2)}) collective-permute-start(bf16[784,448]{1,0:T(8,128)(2,1)S(1)} %fusion.1.refs_0_), channel_id=1, source_target_pairs={{0,2},{1,3},{2,0},{3,1},{4,6},{5,7},{6,4},{7,5},{8,10},{9,11},{10,... | collective-permute-start | bytes 2107400 | tf_op jit(solution)/shard_map/ppermute | solution.py:379
  287.1 51.1 %collective-permute-start.38 = (bf16[784,448]{1,0:T(8,128)(2,1)S(1)}, bf16[784,448]{1,0:T(8,128)(2,1)S(1)}, u32[]{:S(2)}, u32[]{:S(2)}) collective-permute-start(bf16[784,448]{1,0:T(8,128)(2,1)S(1)} %fusion.1.refs_0_), channel_id=1, source_target_pairs={{0,1},{1,0},{2,3},{3,2},{4,5},{5,4},{6,7},{7,6},{8,9},{9,8},{10,11... | collective-permute-start | bytes 2107400 | tf_op jit(solution)/shard_map/ppermute | solution.py:379
  305.6 32.6 %collective-permute-start.39 = (bf16[784,448]{1,0:T(8,128)(2,1)S(1)}, bf16[784,448]{1,0:T(8,128)(2,1)S(1)}, u32[]{:S(2)}, u32[]{:S(2)}) collective-permute-start(bf16[784,448]{1,0:T(8,128)(2,1)S(1)} %collective-permute-done.37.refs_1_), channel_id=1, source_target_pairs={{0,1},{1,0},{2,3},{3,2},{4,5},{5,4},{6,7},{7,6},{8,9},{9,8},{10,11... | collective-permute-start | bytes 2107400 | tf_op jit(solution)/shard_map/ppermute | solution.py:379
  (25 other events, 323.3 us)
where the time goes:
time: 348 us; the launch traced here: 347 us
  Pallas kernels  183 us (53%)
  waiting for transfers between devices  87.3 us (25%)
  starting transfers between devices  58.5 us (17%)
  local copies, waits for them, and re-layouts  11.7 us (3%)
  other arithmetic  5.25 us (2%)
    pallas_call x3, Pallas kernels, enlarge(): pl.pallas_call(functools.partial(enlarge_kernel, layout_of(pieces) if pie...  89.4 us
    ppermute x40, waiting for transfers between devices, swap(): lax.ppermute(x, ('wide', 'narrow'), [(i, i ^ mask) for i in range(count)])  87.3 us
    ppermute x40, starting transfers between devices, swap(): lax.ppermute(x, ('wide', 'narrow'), [(i, i ^ mask) for i in range(count)])  58.5 us
    pallas_call x2, Pallas kernels, project(): pl.pallas_call(functools.partial(project_kernel, layout_of(pieces) if pie...  39.6 us
    pallas_call x1, Pallas kernels, factorize(): pl.pallas_call(functools.partial(factor_kernel, real), out_shape=(jax.Sha...  31.9 us
    pallas_call x1, Pallas kernels, half_left_of(): pl.pallas_call(functools.partial(half_left_kernel, len(lefts)), out_shape...  14 us
    pallas_call x1, Pallas kernels, solve(): pl.pallas_call(functools.partial(solve_kernel, len(pieces)), in_specs=[sm...  7.76 us
  transfers between devices with their start and end apart: 40, of which 22 were waited for; matrix products, arithmetic and copies ran while one was open for 2% of the time, Pallas kernels for 39%

commit v1 on v0

--- a/solution.py
+++ b/solution.py
@@ -11,8 +11,10 @@
 LANES = 128
 BLOCK = 128
 PANEL = 8
-ROWS = 512
-OUTER = ROWS // 64
+GROUP = 8
+OUTER = 8
+ROWS = OUTER * 64
+TIGHT = OUTER * BOND * 8
 SPLIT = 7
 F32 = jnp.float32
 BF16 = jnp.bfloat16
@@ -72,7 +74,7 @@
             begin = pl.multiple_of(begin, 8)
         for c in range(spread.shape[0]):
             data = total[pl.ds(begin, outer), c * LANES:(c + 1) * LANES]
-            spread[c, pl.ds(v * 8 + u, outer, stride=64), :] = data
+            spread[c, pl.ds(v * 8 + u, outer, stride=BOND * 8), :] = data
 
     if outer % 8 == 0:
         lax.fori_loop(0, BOND * BOND, lambda p, carry: (place(p // BOND, p % BOND), carry)[1], 0)
@@ -88,9 +90,9 @@
     width = corners[0].shape[1]
     return pl.pallas_call(
         functools.partial(half_left_kernel, len(lefts)),
-        out_shape=jax.ShapeDtypeStruct((outer * 64, width), BF16),
+        out_shape=jax.ShapeDtypeStruct((outer * BOND * 8, width), BF16),
         scratch_shapes=[pltpu.VMEM((lefts[0].shape[0], -(-width // LANES) * LANES), F32),
-                        pltpu.VMEM((-(-width // LANES), outer * 64, LANES), F32)],
+                        pltpu.VMEM((-(-width // LANES), outer * BOND * 8, LANES), F32)],
         compiler_params=pltpu.CompilerParams(vmem_limit_bytes=60 << 20),
         name="half_left",
     )(*lefts, *corners)
@@ -106,12 +108,14 @@
             assemble(layout, order_ref, pieces, stage, right_all, sems)
     else:
         right_all, _, out_ref, strip, ket = rest
-    rows = half_ref.shape[0]
+    rows = strip.shape[1]
     square = BOND * BOND
     span = BOND * LANES
     half_left = half_ref[...]
     for l in range(BOND):
-        strip[l] = jnp.dot(half_left, right_all[:, l * span:(l + 1) * span], preferred_element_type=F32).astype(BF16)
+        value = jnp.dot(half_left, right_all[:, l * span:(l + 1) * span], preferred_element_type=F32)
+        value = jnp.concatenate([value.reshape(OUTER, BOND * 8, span), jnp.zeros((OUTER, 8, span), F32)], axis=1)
+        strip[l] = value.astype(BF16).reshape(rows, span)
 
     def one_pair(pair, carry):
         for i in range(2):
@@ -162,10 +166,10 @@
     square = BOND * BOND
     lanes = square * LANES
     out_rows = ROWS // 128 * BOND * 16
-    in_specs = [pl.BlockSpec(memory_space=pltpu.SMEM), pl.BlockSpec((ROWS, depth), lambda s: (s + begin, 0)),
+    in_specs = [pl.BlockSpec(memory_space=pltpu.SMEM), pl.BlockSpec((TIGHT, depth), lambda s: (s + begin, 0)),
                 whole_block(first), whole_block(second)]
     out_specs = [pl.BlockSpec((out_rows, lanes), lambda s: (s + begin, 0))]
-    out_shape = [jax.ShapeDtypeStruct((total // ROWS * out_rows, lanes), BF16)]
+    out_shape = [jax.ShapeDtypeStruct((total // TIGHT * out_rows, lanes), BF16)]
     scratch = [pltpu.VMEM((BOND, ROWS, BOND * LANES), BF16), pltpu.VMEM((2, square, 16, BOND * LANES), BF16)]
     if pieces:
         shape = shape_of(pieces)
@@ -258,7 +262,8 @@
         row_b = lax.broadcasted_iota(jnp.int32, (BLOCK, BLOCK), 0)
         lane_b = lax.broadcasted_iota(jnp.int32, (BLOCK, BLOCK), 1)
         cell[:, BLOCK:] = (row_b == lane_b).astype(F32)
-        for p in range(panels):
+
+        def one_panel(p):
             base = p * PANEL
             left = cell[base:base + PANEL, :BLOCK]
             right = cell[base:base + PANEL, BLOCK:]
@@ -274,7 +279,7 @@
                 left = left - factor * jnp.broadcast_to(left[t:t + 1, :], (PANEL, BLOCK))
                 right = right - factor * jnp.broadcast_to(right[t:t + 1, :], (PANEL, BLOCK))
             weights = jnp.transpose(left * scale)
-            for g in range(p + 1, panels):
+            for g in range(p + 1, (p // GROUP + 1) * GROUP):
                 at = slice(g * PANEL, (g + 1) * PANEL)
                 a, b = cell[at, :BLOCK], cell[at, BLOCK:]
                 for t in range(PANEL):
@@ -284,18 +289,37 @@
                 cell[at, :BLOCK] = a
                 cell[at, BLOCK:] = b
             root = jnp.sqrt(scale)
+            cell[base:base + PANEL, :BLOCK] = left * root
             cell[base:base + PANEL, BLOCK:] = right * root
-        low = cell[:, BLOCK:]
-        mine = jnp.dot(low, work[k], precision=HIGHEST, preferred_element_type=F32)
-        work[k] = mine
-
-        def update(i, c):
-            there = pl.ds(pl.multiple_of(i * BLOCK, BLOCK), BLOCK)
-            work[i] = work[i] - lax.dot_general(work[k, :, there], mine, (((0,), (0,)), ((), ())),
-                                                precision=HIGHEST, preferred_element_type=F32)
-            return c
-
-        lax.fori_loop(k + 1, blocks, update, 0)
+            end = base + PANEL
+            if end % (GROUP * PANEL) == 0 and end < BLOCK:
+                done = cell[end - GROUP * PANEL:end, :]
+                change = lax.dot_general(done[:, :BLOCK], done, (((0,), (0,)), ((), ())),
+                                         precision=HIGHEST, preferred_element_type=F32)
+                cell[end:, :] = cell[end:, :] - change[end:, :]
+
+        sure = (real - (blocks - 1) * BLOCK + PANEL - 1) // PANEL
+        for p in range(sure):
+            one_panel(p)
+
+        @pl.when(k < blocks - 1)
+        def _():
+            for p in range(sure, panels):
+                one_panel(p)
+
+        window = pl.ds(pl.multiple_of(k * BLOCK, BLOCK), size + BLOCK)
+        mine = jnp.dot(cell[:, BLOCK:], work[k, :, window], precision=HIGHEST, preferred_element_type=F32)
+        work[k, :, window] = mine
+
+        @pl.when(k < blocks - 1)
+        def _():
+            change = lax.dot_general(mine[:, BLOCK:size], mine, (((0,), (0,)), ((), ())),
+                                     precision=HIGHEST, preferred_element_type=F32)
+            for n in range(blocks - 1):
+                @pl.when(k + 1 + n < blocks)
+                def _():
+                    work[k + 1 + n, :, window] = work[k + 1 + n, :, window] - change[n * BLOCK:(n + 1) * BLOCK]
+
         return carry
 
     lax.fori_loop(0, blocks, block_step, 0)
@@ -336,7 +360,7 @@
     _, outer, cols = out_ref.shape
     low = inverse_ref[pl.ds(pl.multiple_of(own_ref[0] * cols, 8), cols), :]
     terms = []
-    for _ in range(3):
+    for _ in range(2):
         term = low.astype(BF16)
         low = low - term.astype(F32)
         terms.append(term)
@@ -463,7 +487,7 @@
         order = order ^ (me // narrow)
     basis, _ = gather_wide(warm_basis.transpose(0, 2, 1), ahead)
 
-    steps = half_left.shape[0] // ROWS
+    steps = half_left.shape[0] // TIGHT
     cuts = [0, 3, 5, steps] if steps > 5 else [0, steps]
     enlarged = None
     for n in range(len(cuts) - 1):

time: 348 us -> 341 us (0.980)
  Pallas kernels: 183 us -> 170 us
  waiting for transfers between devices: 87.3 us -> 92.9 us
    ppermute x40, waiting for transfers between devices: 87.3 us -> 92.9 us  [swap(): lax.ppermute(x, ('wide', 'narrow'), [(i, i ^ mask) for i in range(count)])]
    pallas_call x1, Pallas kernels: 14 us -> 9.42 us  [half_left_of(): pl.pallas_call(functools.partial(half_left_kernel, len(lefts)), out_shape...]
    pallas_call x1, Pallas kernels: 31.9 us -> 27.9 us  [factorize(): pl.pallas_call(functools.partial(factor_kernel, real), out_shape=(jax.Sha...]
  transfers between devices with their start and end apart: 40 -> 40, of which waited for: 22 -> 22; matrix products, arithmetic and copies ran while one was open for 2% -> 2% of each run, Pallas kernels for 39% -> 36%
where the time goes in v1:
time: 341 us; the launch traced here: 340 us
  Pallas kernels  170 us (50%)
  waiting for transfers between devices  92.9 us (27%)
  starting transfers between devices  58.4 us (17%)
  local copies, waits for them, and re-layouts  11.7 us (3%)
  other arithmetic  5.21 us (2%)
    ppermute x40, waiting for transfers between devices, swap(): lax.ppermute(x, ('wide', 'narrow'), [(i, i ^ mask) for i in range(count)])  92.9 us
    pallas_call x3, Pallas kernels, enlarge(): pl.pallas_call(functools.partial(enlarge_kernel, layout_of(pieces) if pie...  86.4 us
    ppermute x40, starting transfers between devices, swap(): lax.ppermute(x, ('wide', 'narrow'), [(i, i ^ mask) for i in range(count)])  58.4 us
    pallas_call x2, Pallas kernels, project(): pl.pallas_call(functools.partial(project_kernel, layout_of(pieces) if pie...  39.6 us
    pallas_call x1, Pallas kernels, factorize(): pl.pallas_call(functools.partial(factor_kernel, real), out_shape=(jax.Sha...  27.9 us
    pallas_call x1, Pallas kernels, half_left_of(): pl.pallas_call(functools.partial(half_left_kernel, len(lefts)), out_shape...  9.42 us
    pallas_call x1, Pallas kernels, solve(): pl.pallas_call(functools.partial(solve_kernel, len(pieces)), in_specs=[sm...  6.93 us
  transfers between devices with their start and end apart: 40, of which 22 were waited for; matrix products, arithmetic and copies ran while one was open for 2% of the time, Pallas kernels for 36%

profile of v1, /device:TPU:0, one launch (start us, length us, event | category | flops | bytes accessed | tf_op | source)
XLA Modules:
  0.0 340.3 jit_solution(7064208407056716660)
XLA Ops:
  0.6 5.1 %collective-permute-start.9 = (bf16[49,56,112]{2,1,0:T(8,128)(2,1)}, bf16[49,56,112]{2,1,0:T(8,128)(2,1)S(1)}, u32[]{:S(2)}, u32[]{:S(2)}) collective-permute-start(bf16[49,56,112]{2,1,0:T(8,128)(2,1)} %bitcast.126), channel_id=1, source_target_pairs={{0,24},{1,25},{2,26},{3,27},{4,28},{5,29},{6,30},{7,31},{8,16},{9,... | collective-permute-start | bytes 1843976 | tf_op jit(solution)/shard_map/ppermute | solution.py:403
  8.8 13.9 %collective-permute-done.9.rest_6_ = bf16[49,56,112]{2,1,0:T(8,128)(2,1)S(1)} collective-permute-done((bf16[49,56,112]{2,1,0:T(8,128)(2,1)}, bf16[49,56,112]{2,1,0:T(8,128)(2,1)S(1)}, u32[]{:S(2)}, u32[]{:S(2)}) %collective-permute-start.9) | collective-permute-done | bytes 614688 | tf_op jit(solution)/shard_map/ppermute | solution.py:403
  22.7 13.8 %collective-permute-start.10 = (bf16[49,56,112]{2,1,0:T(8,128)(2,1)S(1)}, bf16[49,56,112]{2,1,0:T(8,128)(2,1)}, u32[]{:S(2)}, u32[]{:S(2)}) collective-permute-start(bf16[49,56,112]{2,1,0:T(8,128)(2,1)S(1)} %collective-permute-done.9.rest_6_), channel_id=1, source_target_pairs={{0,8},{1,9},{2,10},{3,11},{4,12},{5,13},{6,14},{7,15},{8,0},{9,1},... | collective-permute-start | bytes 1843976 | tf_op jit(solution)/shard_map/ppermute | solution.py:403
  38.0 3.5 %collective-permute-done.3.refs_5_ = bf16[112,448]{1,0:T(8,128)(2,1)S(1)} collective-permute-done((bf16[112,448]{1,0:T(8,128)(2,1)}, bf16[112,448]{1,0:T(8,128)(2,1)S(1)}, u32[]{:S(2)}, u32[]{:S(2)}) %collective-permute-start.3) | collective-permute-done | bytes 100384 | tf_op jit(solution)/shard_map/ppermute | solution.py:403
  44.9 2.5 collective-permute-start.12
  48.9 3.7 %collective-permute-done.10.rest_4_ = bf16[49,56,112]{2,1,0:T(8,128)(2,1)} collective-permute-done((bf16[49,56,112]{2,1,0:T(8,128)(2,1)S(1)}, bf16[49,56,112]{2,1,0:T(8,128)(2,1)}, u32[]{:S(2)}, u32[]{:S(2)}) %collective-permute-start.10) | collective-permute-done | bytes 614688 | tf_op jit(solution)/shard_map/ppermute | solution.py:403
  56.3 2.2 mul.24.first_ref
  60.8 9.4 %half_left.1.half_ref = bf16[3136,448]{1,0:T(8,128)(2,1)} custom-call(bf16[2744,112]{1,0:T(8,128)(2,1)} %bitcast.115, bf16[2744,112]{1,0:T(8,128)(2,1)} %bitcast.7.refs_1_, bf16[2744,112]{1,0:T(8,128)(2,1)} %bitcast.8.refs_2_, bf16[2744,112]{1,0:T(8,128)(2,1)} %bitcast.9.refs_3_, bf16[112,448]{1,0:T(8,128)(2,1)} %refs_4_.1, bf16[112,448]{1,0:T(8,128)(2,1)} %copy-done.13, ...), custom_call_target="tpu_custom_call" | custom-call | tf_op jit(solution)/shard_map/half_left/pallas_call | solution.py:91
  70.3 10.1 %collective-permute-done.11.rest_5_ = bf16[49,56,112]{2,1,0:T(8,128)(2,1)} collective-permute-done((bf16[49,56,112]{2,1,0:T(8,128)(2,1)}, bf16[49,56,112]{2,1,0:T(8,128)(2,1)}, u32[]{:S(2)}, u32[]{:S(2)}) %collective-permute-start.11) | collective-permute-done | bytes 614688 | tf_op jit(solution)/shard_map/ppermute | solution.py:403
  83.2 37.8 %enlarge.3 = (bf16[3136,6272]{1,0:T(8,128)(2,1)}, bf16[448,6272]{1,0:T(8,128)(2,1)}) custom-call(s32[8]{0:T(128)} %iota_xor_fusion.order_ref, bf16[3136,448]{1,0:T(8,128)(2,1)} %half_left.1.half_ref, bf16[392,224]{1,0:T(8,128)(2,1)} %mul.24.first_ref, bf16[56,112]{1,0:T(8,128)(2,1)} %copy.15.second_ref, bf16[49,56,112]{2,1,0:T(8,128)(2,1)} %bitcast.129, ...), custom_call_target="tpu_custom_call" | custom-call | flops 19730006016 | bytes 16859136 | tf_op jit(solution)/shard_map/enlarge/pallas_call | solution.py:185
  121.1 2.1 collective-permute-start.17
  123.2 24.3 %enlarge.4.rest_1_ = bf16[3136,6272]{1,0:T(8,128)(2,1)} custom-call(s32[8]{0:T(128)} %iota_xor_fusion.order_ref, bf16[3136,448]{1,0:T(8,128)(2,1)} %half_left.1.half_ref, bf16[392,224]{1,0:T(8,128)(2,1)} %mul.24.first_ref, bf16[56,112]{1,0:T(8,128)(2,1)} %copy.15.second_ref, ...), custom_call_target="tpu_custom_call", output_to_operand_aliasing={{}: (5, {})} | custom-call | flops 13153337344 | bytes 11239424 | tf_op jit(solution)/shard_map/enlarge/pallas_call | solution.py:185
  148.1 2.5 collective-permute-start.19
  152.1 24.2 %enlarge.5.rows_ref = bf16[3136,6272]{1,0:T(8,128)(2,1)} custom-call(s32[8]{0:T(128)} %iota_xor_fusion.order_ref, bf16[3136,448]{1,0:T(8,128)(2,1)} %half_left.1.half_ref, bf16[392,224]{1,0:T(8,128)(2,1)} %mul.24.first_ref, bf16[56,112]{1,0:T(8,128)(2,1)} %copy.15.second_ref, ...), custom_call_target="tpu_custom_call", output_to_operand_aliasing={{}: (5, {})} | custom-call | flops 13153337344 | bytes 11239424 | tf_op jit(solution)/shard_map/enlarge/pallas_call | solution.py:185
  176.4 1.9 collective-permute-done.18.refs_5_
  179.1 21.9 %project.2 = (bf16[1568,448]{1,0:T(8,128)(2,1)}, bf16[448,6272]{1,0:T(8,128)(2,1)}) custom-call(s32[8]{0:T(128)} %iota_xor_fusion.order_ref, s32[1]{0:T(128)} %bitcast.14.spot_ref, bf16[3136,6272]{1,0:T(8,128)(2,1)} %enlarge.5.rows_ref, bf16[49,56,112]{2,1,0:T(8,128)(2,1)} %bitcast.109, bf16[49,56,112]{2,1,0:T(8,128)(2,1)} %copy-done.9, ...), custom_call_target="tpu_custom_call" | custom-call | flops 8811708416 | bytes 19668992 | tf_op jit(solution)/shard_map/project/pallas_call | solution.py:229
  202.4 2.3 collective-permute-done.20
  205.0 17.7 %project.3 = bf16[1568,448]{1,0:T(8,128)(2,1)} custom-call(s32[8]{0:T(128)} %iota_xor_fusion.order_ref, s32[1]{0:T(128)} %bitcast.4.spot_ref, bf16[3136,6272]{1,0:T(8,128)(2,1)} %enlarge.5.rows_ref, bf16[448,6272]{1,0:T(8,128)(2,1)} %get-tuple-element.18.refs_0_), custom_call_target="tpu_custom_call" | custom-call | flops 8811708416 | bytes 19668992 | tf_op jit(solution)/shard_map/project/pallas_call | solution.py:229
  222.6 2.2 dynamic-slice_bitcast_fusion
  227.3 17.9 %collective-permute-done.22 = bf16[784,448]{1,0:T(8,128)(2,1)} collective-permute-done((bf16[784,448]{1,0:T(8,128)(2,1)S(1)}, bf16[784,448]{1,0:T(8,128)(2,1)}, u32[]{:S(2)}, u32[]{:S(2)}) %collective-permute-start.22) | collective-permute-done | bytes 702496 | tf_op jit(solution)/shard_map/ppermute | solution.py:403
  253.9 3.2 collective-permute-done.25
  257.2 1.6 collective-permute-start.27
  261.6 2.0 collective-permute-done.28
  263.6 2.3 collective-permute-done.29
  265.9 1.9 collective-permute-start.31
  267.8 2.5 collective-permute-start.32
  270.7 2.7 collective-permute-done.32
  275.4 1.7 collective-permute-start.35
  278.5 2.1 collective-permute-done.35
  284.9 18.5 %collective-permute-done.37.refs_1_ = bf16[784,448]{1,0:T(8,128)(2,1)S(1)} collective-permute-done((bf16[784,448]{1,0:T(8,128)(2,1)S(1)}, bf16[784,448]{1,0:T(8,128)(2,1)S(1)}, u32[]{:S(2)}, u32[]{:S(2)}) %collective-permute-start.37) | collective-permute-done | bytes 702496 | tf_op jit(solution)/shard_map/ppermute | solution.py:403
  304.2 27.9 %factor.1 = (f32[448,448]{1,0:T(8,128)}, f32[448,448]{1,0:T(8,128)}) custom-call(f32[1280,128]{1,0:T(8,128)} %pad_maximum_fusion.gram_ref), custom_call_target="tpu_custom_call" | custom-call | tf_op jit(solution)/shard_map/factor/pallas_call | solution.py:346
  333.2 6.9 %solve.1 = f32[49,56,112]{2,1,0:T(8,128)} custom-call(s32[4]{0:T(128)} %pad_add_fusion.spots_ref, s32[1]{0:T(128)} %bitcast.own_ref, f32[448,448]{1,0:T(8,128)} %get-tuple-element.21.inverse_ref, bf16[784,448]{1,0:T(8,128)(2,1)} %copy-done.1, bf16[784,448]{1,0:T(8,128)(2,1)} %copy-done.3, bf16[784,448]{1,0:T(8,128)(2,1)} %copy-done.4, bf16[784,448]{1,0:T(8,128)(2,1)} %copy-done.5), custom_call_target="tpu_custom_call" | custom-call | tf_op jit(solution)/shard_map/solve/pallas_call | solution.py:390
  (132 shorter events, 46.7 us)
Async XLA Ops:
  0.6 22.0 %collective-permute-start.9 = (bf16[49,56,112]{2,1,0:T(8,128)(2,1)}, bf16[49,56,112]{2,1,0:T(8,128)(2,1)S(1)}, u32[]{:S(2)}, u32[]{:S(2)}) collective-permute-start(bf16[49,56,112]{2,1,0:T(8,128)(2,1)} %bitcast.126), channel_id=1, source_target_pairs={{0,24},{1,25},{2,26},{3,27},{4,28},{5,29},{6,30},{7,31},{8,16},{9,... | collective-permute-start | bytes 1843976 | tf_op jit(solution)/shard_map/ppermute | solution.py:403
  5.8 38.9 %collective-permute-start = (bf16[49,56,112]{2,1,0:T(8,128)(2,1)}, bf16[49,56,112]{2,1,0:T(8,128)(2,1)}, u32[]{:S(2)}, u32[]{:S(2)}) collective-permute-start(bf16[49,56,112]{2,1,0:T(8,128)(2,1)} %bitcast.113), channel_id=1, source_target_pairs={{0,2},{1,3},{2,0},{3,1},{4,6},{5,7},{6,4},{7,5},{8,10},{9,11},{10,... | collective-permute-start | bytes 1843976 | tf_op jit(solution)/shard_map/ppermute | solution.py:403
  7.3 37.6 %collective-permute-start.6 = (bf16[49,56,112]{2,1,0:T(8,128)(2,1)}, bf16[49,56,112]{2,1,0:T(8,128)(2,1)}, u32[]{:S(2)}, u32[]{:S(2)}) collective-permute-start(bf16[49,56,112]{2,1,0:T(8,128)(2,1)} %bitcast.127), channel_id=1, source_target_pairs={{0,4},{1,5},{2,6},{3,7},{4,0},{5,1},{6,2},{7,3},{8,12},{9,13},{10,... | collective-permute-start | bytes 1843976 | tf_op jit(solution)/shard_map/ppermute | solution.py:403
  8.8 38.6 %collective-permute-start.7 = (bf16[49,56,112]{2,1,0:T(8,128)(2,1)}, bf16[49,56,112]{2,1,0:T(8,128)(2,1)}, u32[]{:S(2)}, u32[]{:S(2)}) collective-permute-start(bf16[49,56,112]{2,1,0:T(8,128)(2,1)} %bitcast.128), channel_id=1, source_target_pairs={{0,8},{1,9},{2,10},{3,11},{4,12},{5,13},{6,14},{7,15},{8,0},{9,1},... | collective-permute-start | bytes 1843976 | tf_op jit(solution)/shard_map/ppermute | solution.py:403
  22.7 30.0 %collective-permute-start.10 = (bf16[49,56,112]{2,1,0:T(8,128)(2,1)S(1)}, bf16[49,56,112]{2,1,0:T(8,128)(2,1)}, u32[]{:S(2)}, u32[]{:S(2)}) collective-permute-start(bf16[49,56,112]{2,1,0:T(8,128)(2,1)S(1)} %collective-permute-done.9.rest_6_), channel_id=1, source_target_pairs={{0,8},{1,9},{2,10},{3,11},{4,12},{5,13},{6,14},{7,15},{8,0},{9,1},... | collective-permute-start | bytes 1843976 | tf_op jit(solution)/shard_map/ppermute | solution.py:403
  36.5 5.0 %collective-permute-start.3 = (bf16[112,448]{1,0:T(8,128)(2,1)}, bf16[112,448]{1,0:T(8,128)(2,1)S(1)}, u32[]{:S(2)}, u32[]{:S(2)}) collective-permute-start(bf16[112,448]{1,0:T(8,128)(2,1)} %refs_4_.1), channel_id=1, source_target_pairs={{0,2},{1,3},{2,0},{3,1},{4,6},{5,7},{6,4},{7,5},{8,10},{9,11},{10,... | collective-permute-start | bytes 301064 | tf_op jit(solution)/shard_map/ppermute | solution.py:403
  44.4 16.5 %collective-permute-start.1 = (bf16[49,56,112]{2,1,0:T(8,128)(2,1)}, bf16[49,56,112]{2,1,0:T(8,128)(2,1)}, u32[]{:S(2)}, u32[]{:S(2)}) collective-permute-start(bf16[49,56,112]{2,1,0:T(8,128)(2,1)} %bitcast.114), channel_id=1, source_target_pairs={{0,1},{1,0},{2,3},{3,2},{4,5},{5,4},{6,7},{7,6},{8,9},{9,8},{10,11... | collective-permute-start | bytes 1843976 | tf_op jit(solution)/shard_map/ppermute | solution.py:403
  44.6 16.2 %collective-permute-start.2 = (bf16[49,56,112]{2,1,0:T(8,128)(2,1)}, bf16[49,56,112]{2,1,0:T(8,128)(2,1)}, u32[]{:S(2)}, u32[]{:S(2)}) collective-permute-start(bf16[49,56,112]{2,1,0:T(8,128)(2,1)} %collective-permute-done), channel_id=1, source_target_pairs={{0,1},{1,0},{2,3},{3,2},{4,5},{5,4},{6,7},{7,6},{8,9},{9,8},{10,11... | collective-permute-start | bytes 1843976 | tf_op jit(solution)/shard_map/ppermute | solution.py:403
  44.9 25.4 %collective-permute-start.12 = (bf16[49,56,112]{2,1,0:T(8,128)(2,1)}, bf16[49,56,112]{2,1,0:T(8,128)(2,1)}, u32[]{:S(2)}, u32[]{:S(2)}) collective-permute-start(bf16[49,56,112]{2,1,0:T(8,128)(2,1)} %collective-permute-done.6.rest_1_), channel_id=1, source_target_pairs={{0,24},{1,25},{2,26},{3,27},{4,28},{5,29},{6,30},{7,31},{8,16},{9,... | collective-permute-start | bytes 1843976 | tf_op jit(solution)/shard_map/ppermute | solution.py:403
  47.4 22.9 %collective-permute-start.8 = (bf16[49,56,112]{2,1,0:T(8,128)(2,1)}, bf16[49,56,112]{2,1,0:T(8,128)(2,1)}, u32[]{:S(2)}, u32[]{:S(2)}) collective-permute-start(bf16[49,56,112]{2,1,0:T(8,128)(2,1)} %collective-permute-done.7.rest_2_), channel_id=1, source_target_pairs={{0,4},{1,5},{2,6},{3,7},{4,0},{5,1},{6,2},{7,3},{8,12},{9,13},{10,... | collective-permute-start | bytes 1843976 | tf_op jit(solution)/shard_map/ppermute | solution.py:403
  52.6 27.7 %collective-permute-start.11 = (bf16[49,56,112]{2,1,0:T(8,128)(2,1)}, bf16[49,56,112]{2,1,0:T(8,128)(2,1)}, u32[]{:S(2)}, u32[]{:S(2)}) collective-permute-start(bf16[49,56,112]{2,1,0:T(8,128)(2,1)} %collective-permute-done.10.rest_4_), channel_id=1, source_target_pairs={{0,4},{1,5},{2,6},{3,7},{4,0},{5,1},{6,2},{7,3},{8,12},{9,13},{10,... | collective-permute-start | bytes 1843976 | tf_op jit(solution)/shard_map/ppermute | solution.py:403
  80.4 40.7 %collective-permute-start.16 = (bf16[49,56,112]{2,1,0:T(8,128)(2,1)S(1)}, bf16[49,56,112]{2,1,0:T(8,128)(2,1)S(1)}, u32[]{:S(2)}, u32[]{:S(2)}) collective-permute-start(bf16[49,56,112]{2,1,0:T(8,128)(2,1)S(1)} %bitcast.110), channel_id=1, source_target_pairs={{0,24},{1,25},{2,26},{3,27},{4,28},{5,29},{6,30},{7,31},{8,16},{9,... | collective-permute-start | bytes 1843976 | tf_op jit(solution)/shard_map/ppermute | solution.py:403
  81.7 65.8 %collective-permute-start.14 = (bf16[49,56,112]{2,1,0:T(8,128)(2,1)S(1)}, bf16[49,56,112]{2,1,0:T(8,128)(2,1)S(1)}, u32[]{:S(2)}, u32[]{:S(2)}) collective-permute-start(bf16[49,56,112]{2,1,0:T(8,128)(2,1)S(1)} %bitcast.111), channel_id=1, source_target_pairs={{0,8},{1,9},{2,10},{3,11},{4,12},{5,13},{6,14},{7,15},{8,0},{9,1},... | collective-permute-start | bytes 1843976 | tf_op jit(solution)/shard_map/ppermute | solution.py:403
  81.7 66.4 %collective-permute-start.13 = (bf16[49,56,112]{2,1,0:T(8,128)(2,1)S(1)}, bf16[49,56,112]{2,1,0:T(8,128)(2,1)S(1)}, u32[]{:S(2)}, u32[]{:S(2)}) collective-permute-start(bf16[49,56,112]{2,1,0:T(8,128)(2,1)S(1)} %bitcast.112), channel_id=1, source_target_pairs={{0,4},{1,5},{2,6},{3,7},{4,0},{5,1},{6,2},{7,3},{8,12},{9,13},{10,... | collective-permute-start | bytes 1843976 | tf_op jit(solution)/shard_map/ppermute | solution.py:403
  121.1 29.4 %collective-permute-start.17 = (bf16[49,56,112]{2,1,0:T(8,128)(2,1)S(1)}, bf16[49,56,112]{2,1,0:T(8,128)(2,1)S(1)}, u32[]{:S(2)}, u32[]{:S(2)}) collective-permute-start(bf16[49,56,112]{2,1,0:T(8,128)(2,1)S(1)} %collective-permute-done.16.refs_6_), channel_id=1, source_target_pairs={{0,8},{1,9},{2,10},{3,11},{4,12},{5,13},{6,14},{7,15},{8,0},{9,1},... | collective-permute-start | bytes 1843976 | tf_op jit(solution)/shard_map/ppermute | solution.py:403
  147.5 28.8 %collective-permute-start.15 = (bf16[49,56,112]{2,1,0:T(8,128)(2,1)S(1)}, bf16[49,56,112]{2,1,0:T(8,128)(2,1)}, u32[]{:S(2)}, u32[]{:S(2)}) collective-permute-start(bf16[49,56,112]{2,1,0:T(8,128)(2,1)S(1)} %collective-permute-done.14.refs_2_), channel_id=1, source_target_pairs={{0,4},{1,5},{2,6},{3,7},{4,0},{5,1},{6,2},{7,3},{8,12},{9,13},{10,... | collective-permute-start | bytes 1843976 | tf_op jit(solution)/shard_map/ppermute | solution.py:403
  148.1 28.3 %collective-permute-start.19 = (bf16[49,56,112]{2,1,0:T(8,128)(2,1)S(1)}, bf16[49,56,112]{2,1,0:T(8,128)(2,1)S(1)}, u32[]{:S(2)}, u32[]{:S(2)}) collective-permute-start(bf16[49,56,112]{2,1,0:T(8,128)(2,1)S(1)} %collective-permute-done.13.refs_1_), channel_id=1, source_target_pairs={{0,24},{1,25},{2,26},{3,27},{4,28},{5,29},{6,30},{7,31},{8,16},{9,... | collective-permute-start | bytes 1843976 | tf_op jit(solution)/shard_map/ppermute | solution.py:403
  150.5 27.7 %collective-permute-start.18 = (bf16[49,56,112]{2,1,0:T(8,128)(2,1)S(1)}, bf16[49,56,112]{2,1,0:T(8,128)(2,1)S(1)}, u32[]{:S(2)}, u32[]{:S(2)}) collective-permute-start(bf16[49,56,112]{2,1,0:T(8,128)(2,1)S(1)} %collective-permute-done.17.refs_4_), channel_id=1, source_target_pairs={{0,4},{1,5},{2,6},{3,7},{4,0},{5,1},{6,2},{7,3},{8,12},{9,13},{10,... | collective-permute-start | bytes 1843976 | tf_op jit(solution)/shard_map/ppermute | solution.py:403
  225.0 20.3 %collective-permute-start.22 = (bf16[784,448]{1,0:T(8,128)(2,1)S(1)}, bf16[784,448]{1,0:T(8,128)(2,1)}, u32[]{:S(2)}, u32[]{:S(2)}) collective-permute-start(bf16[784,448]{1,0:T(8,128)(2,1)S(1)} %fusion.2), channel_id=1, source_target_pairs={{0,2},{1,3},{2,0},{3,1},{4,6},{5,7},{6,4},{7,5},{8,10},{9,11},{10,... | collective-permute-start | bytes 2107400 | tf_op jit(solution)/shard_map/ppermute | solution.py:403
  249.4 4.6 %collective-permute-start.24 = (f32[160,128]{1,0:T(8,128)S(1)}, f32[160,128]{1,0:T(8,128)S(1)}, u32[]{:S(2)}, u32[]{:S(2)}) collective-permute-start(f32[160,128]{1,0:T(8,128)S(1)} %get-tuple-element.32), channel_id=1, source_target_pairs={{0,2},{1,3},{2,0},{3,1},{4,6},{5,7},{6,4},{7,5},{8,10},{9,11},{10,... | collective-permute-start | bytes 245768 | tf_op jit(solution)/shard_map/ppermute | solution.py:403
  250.9 6.2 %collective-permute-start.25 = (f32[160,128]{1,0:T(8,128)S(1)}, f32[160,128]{1,0:T(8,128)S(1)}, u32[]{:S(2)}, u32[]{:S(2)}) collective-permute-start(f32[160,128]{1,0:T(8,128)S(1)} %get-tuple-element.34), channel_id=1, source_target_pairs={{0,4},{1,5},{2,6},{3,7},{4,0},{5,1},{6,2},{7,3},{8,12},{9,13},{10,... | collective-permute-start | bytes 245768 | tf_op jit(solution)/shard_map/ppermute | solution.py:403
  251.4 5.7 %collective-permute-start.26 = (f32[160,128]{1,0:T(8,128)S(1)}, f32[160,128]{1,0:T(8,128)S(1)}, u32[]{:S(2)}, u32[]{:S(2)}) collective-permute-start(f32[160,128]{1,0:T(8,128)S(1)} %get-tuple-element.33), channel_id=1, source_target_pairs={{0,6},{1,7},{2,4},{3,5},{4,2},{5,3},{6,0},{7,1},{8,14},{9,15},{10,... | collective-permute-start | bytes 245768 | tf_op jit(solution)/shard_map/ppermute | solution.py:403
  257.2 4.5 %collective-permute-start.27 = (f32[40,128]{1,0:T(8,128)S(1)}, f32[40,128]{1,0:T(8,128)S(1)}, u32[]{:S(2)}, u32[]{:S(2)}) collective-permute-start(f32[40,128]{1,0:T(8,128)S(1)} %get-tuple-element.41), channel_id=1, source_target_pairs={{0,8},{1,9},{2,10},{3,11},{4,12},{5,13},{6,14},{7,15},{8,0},{9,1},... | collective-permute-start | bytes 61448 | tf_op jit(solution)/shard_map/ppermute | solution.py:403
  258.8 4.8 %collective-permute-start.28 = (f32[40,128]{1,0:T(8,128)S(1)}, f32[40,128]{1,0:T(8,128)S(1)}, u32[]{:S(2)}, u32[]{:S(2)}) collective-permute-start(f32[40,128]{1,0:T(8,128)S(1)} %get-tuple-element.43), channel_id=1, source_target_pairs={{0,16},{1,17},{2,18},{3,19},{4,20},{5,21},{6,22},{7,23},{8,24},{9,... | collective-permute-start | bytes 61448 | tf_op jit(solution)/shard_map/ppermute | solution.py:403
  260.3 5.6 %collective-permute-start.29 = (f32[40,128]{1,0:T(8,128)S(1)}, f32[40,128]{1,0:T(8,128)S(1)}, u32[]{:S(2)}, u32[]{:S(2)}) collective-permute-start(f32[40,128]{1,0:T(8,128)S(1)} %get-tuple-element.42), channel_id=1, source_target_pairs={{0,24},{1,25},{2,26},{3,27},{4,28},{5,29},{6,30},{7,31},{8,16},{9,... | collective-permute-start | bytes 61448 | tf_op jit(solution)/shard_map/ppermute | solution.py:403
  265.9 4.7 %collective-permute-start.31 = (f32[40,128]{1,0:T(8,128)S(1)}, f32[40,128]{1,0:T(8,128)S(1)}, u32[]{:S(2)}, u32[]{:S(2)}) collective-permute-start(f32[40,128]{1,0:T(8,128)S(1)} %fusion.13), channel_id=1, source_target_pairs={{0,16},{1,17},{2,18},{3,19},{4,20},{5,21},{6,22},{7,23},{8,24},{9,... | collective-permute-start | bytes 61448 | tf_op jit(solution)/shard_map/ppermute | solution.py:403
  267.8 5.6 %collective-permute-start.32 = (f32[40,128]{1,0:T(8,128)S(1)}, f32[40,128]{1,0:T(8,128)S(1)}, u32[]{:S(2)}, u32[]{:S(2)}) collective-permute-start(f32[40,128]{1,0:T(8,128)S(1)} %fusion.13), channel_id=1, source_target_pairs={{0,24},{1,25},{2,26},{3,27},{4,28},{5,29},{6,30},{7,31},{8,16},{9,... | collective-permute-start | bytes 61448 | tf_op jit(solution)/shard_map/ppermute | solution.py:403
  273.5 4.5 %collective-permute-start.33 = (f32[160,128]{1,0:T(8,128)S(1)}, f32[160,128]{1,0:T(8,128)S(1)}, u32[]{:S(2)}, u32[]{:S(2)}) collective-permute-start(f32[160,128]{1,0:T(8,128)S(1)} %get-tuple-element.36), channel_id=1, source_target_pairs={{0,2},{1,3},{2,0},{3,1},{4,6},{5,7},{6,4},{7,5},{8,10},{9,11},{10,... | collective-permute-start | bytes 245768 | tf_op jit(solution)/shard_map/ppermute | solution.py:403
  275.4 5.3 %collective-permute-start.35 = (f32[160,128]{1,0:T(8,128)S(1)}, f32[160,128]{1,0:T(8,128)S(1)}, u32[]{:S(2)}, u32[]{:S(2)}) collective-permute-start(f32[160,128]{1,0:T(8,128)S(1)} %get-tuple-element.36), channel_id=1, source_target_pairs={{0,6},{1,7},{2,4},{3,5},{4,2},{5,3},{6,0},{7,1},{8,14},{9,15},{10,... | collective-permute-start | bytes 245768 | tf_op jit(solution)/shard_map/ppermute | solution.py:403
  283.5 19.9 %collective-permute-start.37 = (bf16[784,448]{1,0:T(8,128)(2,1)S(1)}, bf16[784,448]{1,0:T(8,128)(2,1)S(1)}, u32[]{:S(2)}, u32[]{:S(2)}) collective-permute-start(bf16[784,448]{1,0:T(8,128)(2,1)S(1)} %fusion.1.refs_0_), channel_id=1, source_target_pairs={{0,2},{1,3},{2,0},{3,1},{4,6},{5,7},{6,4},{7,5},{8,10},{9,11},{10,... | collective-permute-start | bytes 2107400 | tf_op jit(solution)/shard_map/ppermute | solution.py:403
  284.9 47.1 %collective-permute-start.38 = (bf16[784,448]{1,0:T(8,128)(2,1)S(1)}, bf16[784,448]{1,0:T(8,128)(2,1)S(1)}, u32[]{:S(2)}, u32[]{:S(2)}) collective-permute-start(bf16[784,448]{1,0:T(8,128)(2,1)S(1)} %fusion.1.refs_0_), channel_id=1, source_target_pairs={{0,1},{1,0},{2,3},{3,2},{4,5},{5,4},{6,7},{7,6},{8,9},{9,8},{10,11... | collective-permute-start | bytes 2107400 | tf_op jit(solution)/shard_map/ppermute | solution.py:403
  303.5 28.6 %collective-permute-start.39 = (bf16[784,448]{1,0:T(8,128)(2,1)S(1)}, bf16[784,448]{1,0:T(8,128)(2,1)S(1)}, u32[]{:S(2)}, u32[]{:S(2)}) collective-permute-start(bf16[784,448]{1,0:T(8,128)(2,1)S(1)} %collective-permute-done.37.refs_1_), channel_id=1, source_target_pairs={{0,1},{1,0},{2,3},{3,2},{4,5},{5,4},{6,7},{7,6},{8,9},{9,8},{10,11... | collective-permute-start | bytes 2107400 | tf_op jit(solution)/shard_map/ppermute | solution.py:403
  (25 other events, 316.7 us)

commit v2 on v1

--- a/solution.py
+++ b/solution.py
@@ -54,7 +54,7 @@
             target[pl.ds(pair * 2 * depth, 2 * depth), lane] = joined.astype(BF16)
         return carry
 
-    lax.fori_loop(0, square, fill, 0)
+    lax.fori_loop(0, square, fill, 0, unroll=BOND)
 
 
 def half_left_kernel(parts_of, *refs):
@@ -199,15 +199,21 @@
 def project_kernel(layout, order_ref, spot_ref, rows_ref, *refs):
     count = len(layout)
     if count:
-        pieces, (out_ref, basis_all, stage, sems) = refs[:count], refs[count:]
+        pieces, (mine_ref, other_ref, basis_all, stage, sems) = refs[:count], refs[count:]
 
         @pl.when(pl.program_id(0) == 0)
         def _():
             assemble(layout, order_ref, pieces, stage, basis_all, sems)
     else:
-        basis_all, out_ref = refs
-    out_ref[...] = lax.dot_general(rows_ref[...], basis_all[...], (((1,), (1,)), ((), ())),
-                                   preferred_element_type=F32).astype(out_ref.dtype)
+        basis_all, mine_ref, other_ref = refs
+    value = lax.dot_general(rows_ref[...], basis_all[...], (((1,), (1,)), ((), ())),
+                            preferred_element_type=F32).astype(BF16)
+    chunk = value.shape[0] // 2
+    for upper, (low_ref, high_ref) in enumerate(((mine_ref, other_ref), (other_ref, mine_ref))):
+        @pl.when(spot_ref[1] == upper)
+        def _():
+            low_ref[...] = value[:chunk]
+            high_ref[...] = value[chunk:]
 
 
 def project(enlarged, basis, order, spot, rows, width):
@@ -216,8 +222,8 @@
     once = rows // SPLIT
     full = lambda shape: pl.BlockSpec(shape, lambda s, order, spot: (0,) * len(shape), pipeline_mode=pl.Buffered(1))
     in_specs = [pl.BlockSpec((once, lanes), lambda s, order, spot: (spot[0] * SPLIT + s, 0))]
-    out_specs = [pl.BlockSpec((once, width), lambda s, order, spot: (s, 0))]
-    out_shape = [jax.ShapeDtypeStruct((rows, width), BF16)]
+    out_specs = [pl.BlockSpec((once // 2, width), lambda s, order, spot: (s, 0))] * 2
+    out_shape = [jax.ShapeDtypeStruct((rows // 2, width), BF16)] * 2
     scratch = []
     if pieces:
         in_specs += [pl.BlockSpec(memory_space=pl.ANY)] * len(pieces)
@@ -368,10 +374,15 @@
         copy.wait()
     rows = stage.shape[1]
 
+    chunk = rows // SPLIT
+
     def one_part(n, carry):
         data = stage[n]
-        value[pl.ds(pl.multiple_of(n * rows, 8), rows), :] = sum(
-            lax.dot_general(data, term, (((1,), (1,)), ((), ())), preferred_element_type=F32) for term in terms)
+        product = sum(lax.dot_general(data, term, (((1,), (1,)), ((), ())), preferred_element_type=F32)
+                      for term in terms)
+        for s in range(SPLIT):
+            at = (n // 2) * 2 * rows + (2 * s + n % 2) * chunk
+            value[pl.ds(pl.multiple_of(at, 8), chunk), :] = product[s * chunk:(s + 1) * chunk]
         return carry
 
     lax.fori_loop(0, count, one_part, 0)
@@ -499,24 +510,27 @@
     half = enlarged.shape[0] // 2
     spot = lambda *masks: jnp.stack([own ^ m for m in masks])
 
-    def summed(product):
-        parts = product.reshape(2, half // 2, breadth)
-        mine = lax.dynamic_index_in_dim(parts, own % 2, 0, False)
-        other = swap(lax.dynamic_index_in_dim(parts, 1 - own % 2, 0, False), 1)
-        return mine.astype(F32) + other.astype(F32)
-
-    product, basis = project(enlarged, basis, order, (1 - own // 2)[None], half, breadth)
-    near = summed(product).astype(BF16)
+    def summed(mine, other):
+        return mine.astype(F32) + swap(other, 1).astype(F32)
+
+    place = lambda half: jnp.stack([half, own % 2])
+    mine, other, basis = project(enlarged, basis, order, place(1 - own // 2), half, breadth)
+    near = summed(mine, other).astype(BF16)
     enlarged, near = lax.optimization_barrier((enlarged, near))
     near = swap(near, 2)
-    product = project(enlarged, basis, order, (own // 2)[None], half, breadth)
-    rows = (summed(product[0]) + near.astype(F32)).astype(BF16)
+    mine, other = project(enlarged, basis, order, place(own // 2), half, breadth)
+    rows = (summed(mine, other) + near.astype(F32)).astype(BF16)
 
     gram = lax.dot_general(rows, rows, (((0,), (0,)), ((), ())), preferred_element_type=F32) / (breadth * square)
     gram = packed_blocks(gram)
-    for group in groups():
+    *halving, last = groups()
+    for group in halving:
         gram = sum_group(gram, group, me)
-    for group in reversed(groups()):
+    terms = [gram] + [swap(gram, mask) for mask in place_in(last, me)[1][1:]]
+    while len(terms) > 1:
+        terms = [a + b for a, b in zip(terms[::2], terms[1::2])]
+    gram, = terms
+    for group in reversed(halving):
         gram = join_group(gram, group, me)
     rows, gram = lax.optimization_barrier((rows, gram))
     pieces = gather_narrow(rows)

time: 341 us -> 332 us (0.974)
  starting transfers between devices: 58.4 us -> 54 us
  local copies, waits for them, and re-layouts: 11.7 us -> 8.17 us
    ppermute x40 -> x37, starting transfers between devices: 58.4 us -> 54 us  [swap(): lax.ppermute(x, ('wide', 'narrow'), [(i, i ^ mask) for i in range(count)])]
    squeeze x2 -> x0, local copies, waits for them, and re-layouts: 3.51 us -> none  [summed(): other = swap(lax.dynamic_index_in_dim(parts, 1 - own % 2, 0, False), 1)]
    ppermute x40 -> x37, waiting for transfers between devices: 92.9 us -> 89.5 us  [swap(): lax.ppermute(x, ('wide', 'narrow'), [(i, i ^ mask) for i in range(count)])]
  transfers between devices with their start and end apart: 40 -> 37, of which waited for: 22 -> 20; matrix products, arithmetic and copies ran while one was open for 2% -> 3% of each run, Pallas kernels for 36% -> 37%
where the time goes in v2:
time: 332 us; the launch traced here: 331 us
  Pallas kernels  170 us (51%)
  waiting for transfers between devices  89.5 us (27%)
  starting transfers between devices  54 us (16%)
  local copies, waits for them, and re-layouts  8.17 us (2%)
  other arithmetic  7.62 us (2%)
    ppermute x37, waiting for transfers between devices, swap(): lax.ppermute(x, ('wide', 'narrow'), [(i, i ^ mask) for i in range(count)])  89.5 us
    pallas_call x3, Pallas kernels, enlarge(): pl.pallas_call(functools.partial(enlarge_kernel, layout_of(pieces) if pie...  86.1 us
    ppermute x37, starting transfers between devices, swap(): lax.ppermute(x, ('wide', 'narrow'), [(i, i ^ mask) for i in range(count)])  54 us
    pallas_call x2, Pallas kernels, project(): pl.pallas_call(functools.partial(project_kernel, layout_of(pieces) if pie...  39.6 us
    pallas_call x1, Pallas kernels, factorize(): pl.pallas_call(functools.partial(factor_kernel, real), out_shape=(jax.Sha...  27.8 us
    pallas_call x1, Pallas kernels, half_left_of(): pl.pallas_call(functools.partial(half_left_kernel, len(lefts)), out_shape...  9.46 us
    pallas_call x1, Pallas kernels, solve(): pl.pallas_call(functools.partial(solve_kernel, len(pieces)), in_specs=[sm...  6.93 us
  transfers between devices with their start and end apart: 37, of which 20 were waited for; matrix products, arithmetic and copies ran while one was open for 3% of the time, Pallas kernels for 37%

profile of v2, /device:TPU:0, one launch (start us, length us, event | category | flops | bytes accessed | tf_op | source)
XLA Modules:
  0.0 331.1 jit_solution(7314635021050559872)
XLA Ops:
  0.6 5.1 %collective-permute-start.9 = (bf16[49,56,112]{2,1,0:T(8,128)(2,1)}, bf16[49,56,112]{2,1,0:T(8,128)(2,1)S(1)}, u32[]{:S(2)}, u32[]{:S(2)}) collective-permute-start(bf16[49,56,112]{2,1,0:T(8,128)(2,1)} %bitcast.80), channel_id=1, source_target_pairs={{0,24},{1,25},{2,26},{3,27},{4,28},{5,29},{6,30},{7,31},{8,16},{9,... | collective-permute-start | bytes 1843976 | tf_op jit(solution)/shard_map/ppermute | solution.py:414
  7.3 1.5 collective-permute-start.6
  8.8 13.9 %collective-permute-done.9.rest_6_ = bf16[49,56,112]{2,1,0:T(8,128)(2,1)S(1)} collective-permute-done((bf16[49,56,112]{2,1,0:T(8,128)(2,1)}, bf16[49,56,112]{2,1,0:T(8,128)(2,1)S(1)}, u32[]{:S(2)}, u32[]{:S(2)}) %collective-permute-start.9) | collective-permute-done | bytes 614688 | tf_op jit(solution)/shard_map/ppermute | solution.py:414
  22.7 13.8 %collective-permute-start.10 = (bf16[49,56,112]{2,1,0:T(8,128)(2,1)S(1)}, bf16[49,56,112]{2,1,0:T(8,128)(2,1)}, u32[]{:S(2)}, u32[]{:S(2)}) collective-permute-start(bf16[49,56,112]{2,1,0:T(8,128)(2,1)S(1)} %collective-permute-done.9.rest_6_), channel_id=1, source_target_pairs={{0,8},{1,9},{2,10},{3,11},{4,12},{5,13},{6,14},{7,15},{8,0},{9,1},... | collective-permute-start | bytes 1843976 | tf_op jit(solution)/shard_map/ppermute | solution.py:414
  38.0 3.5 %collective-permute-done.3.refs_5_ = bf16[112,448]{1,0:T(8,128)(2,1)S(1)} collective-permute-done((bf16[112,448]{1,0:T(8,128)(2,1)}, bf16[112,448]{1,0:T(8,128)(2,1)S(1)}, u32[]{:S(2)}, u32[]{:S(2)}) %collective-permute-start.3) | collective-permute-done | bytes 100384 | tf_op jit(solution)/shard_map/ppermute | solution.py:414
  44.9 2.5 collective-permute-start.12
  47.4 1.5 collective-permute-start.8
  48.9 3.7 %collective-permute-done.10.rest_4_ = bf16[49,56,112]{2,1,0:T(8,128)(2,1)} collective-permute-done((bf16[49,56,112]{2,1,0:T(8,128)(2,1)S(1)}, bf16[49,56,112]{2,1,0:T(8,128)(2,1)}, u32[]{:S(2)}, u32[]{:S(2)}) %collective-permute-start.10) | collective-permute-done | bytes 614688 | tf_op jit(solution)/shard_map/ppermute | solution.py:414
  52.6 1.5 collective-permute-start.11
  55.3 2.2 mul.24.first_ref
  60.4 9.5 %half_left.1.half_ref = bf16[3136,448]{1,0:T(8,128)(2,1)} custom-call(bf16[2744,112]{1,0:T(8,128)(2,1)} %bitcast.74, bf16[2744,112]{1,0:T(8,128)(2,1)} %bitcast.8.refs_1_, bf16[2744,112]{1,0:T(8,128)(2,1)} %bitcast.9.refs_2_, bf16[2744,112]{1,0:T(8,128)(2,1)} %bitcast.10.refs_3_, bf16[112,448]{1,0:T(8,128)(2,1)} %refs_4_.1, bf16[112,448]{1,0:T(8,128)(2,1)} %copy-done.11, ...), custom_call_target="tpu_custom_call" | custom-call | tf_op jit(solution)/shard_map/half_left/pallas_call | solution.py:91
  69.9 10.4 %collective-permute-done.11.rest_5_ = bf16[49,56,112]{2,1,0:T(8,128)(2,1)} collective-permute-done((bf16[49,56,112]{2,1,0:T(8,128)(2,1)}, bf16[49,56,112]{2,1,0:T(8,128)(2,1)}, u32[]{:S(2)}, u32[]{:S(2)}) %collective-permute-start.11) | collective-permute-done | bytes 614688 | tf_op jit(solution)/shard_map/ppermute | solution.py:414
  83.2 37.5 %enlarge.3 = (bf16[3136,6272]{1,0:T(8,128)(2,1)}, bf16[448,6272]{1,0:T(8,128)(2,1)}) custom-call(s32[8]{0:T(128)} %iota_xor_fusion.order_ref, bf16[3136,448]{1,0:T(8,128)(2,1)} %half_left.1.half_ref, bf16[392,224]{1,0:T(8,128)(2,1)} %mul.24.first_ref, bf16[56,112]{1,0:T(8,128)(2,1)} %copy.15.second_ref, bf16[49,56,112]{2,1,0:T(8,128)(2,1)} %bitcast.83, ...), custom_call_target="tpu_custom_call" | custom-call | flops 19730006016 | bytes 16859136 | tf_op jit(solution)/shard_map/enlarge/pallas_call | solution.py:185
  120.8 2.1 collective-permute-start.17
  122.9 24.3 %enlarge.4.rest_1_ = bf16[3136,6272]{1,0:T(8,128)(2,1)} custom-call(s32[8]{0:T(128)} %iota_xor_fusion.order_ref, bf16[3136,448]{1,0:T(8,128)(2,1)} %half_left.1.half_ref, bf16[392,224]{1,0:T(8,128)(2,1)} %mul.24.first_ref, bf16[56,112]{1,0:T(8,128)(2,1)} %copy.15.second_ref, ...), custom_call_target="tpu_custom_call", output_to_operand_aliasing={{}: (5, {})} | custom-call | flops 13153337344 | bytes 11239424 | tf_op jit(solution)/shard_map/enlarge/pallas_call | solution.py:185
  147.7 2.5 collective-permute-start.19
  151.7 24.3 %enlarge.5.rows_ref = bf16[3136,6272]{1,0:T(8,128)(2,1)} custom-call(s32[8]{0:T(128)} %iota_xor_fusion.order_ref, bf16[3136,448]{1,0:T(8,128)(2,1)} %half_left.1.half_ref, bf16[392,224]{1,0:T(8,128)(2,1)} %mul.24.first_ref, bf16[56,112]{1,0:T(8,128)(2,1)} %copy.15.second_ref, ...), custom_call_target="tpu_custom_call", output_to_operand_aliasing={{}: (5, {})} | custom-call | flops 13153337344 | bytes 11239424 | tf_op jit(solution)/shard_map/enlarge/pallas_call | solution.py:185
  176.0 1.8 collective-permute-done.18.refs_5_
  178.8 21.8 %project.2 = (bf16[784,448]{1,0:T(8,128)(2,1)}, bf16[784,448]{1,0:T(8,128)(2,1)}, bf16[448,6272]{1,0:T(8,128)(2,1)}) custom-call(s32[8]{0:T(128)} %iota_xor_fusion.order_ref, s32[2]{0:T(128)} %pad_add_fusion.2.spot_ref, bf16[3136,6272]{1,0:T(8,128)(2,1)} %enlarge.5.rows_ref, bf16[49,56,112]{2,1,0:T(8,128)(2,1)} %bitcast.68, bf16[49,56,112]{2,1,0:T(8,128)(2,1)} %copy-done.7, ...), custom_call_target="tpu_custom_call" | custom-call | flops 8811708416 | bytes 19668992 | tf_op jit(solution)/shard_map/project/pallas_call | solution.py:235
  201.3 1.9 collective-permute-done.20
  204.6 17.7 %project.3 = (bf16[784,448]{1,0:T(8,128)(2,1)}, bf16[784,448]{1,0:T(8,128)(2,1)}) custom-call(s32[8]{0:T(128)} %iota_xor_fusion.order_ref, s32[2]{0:T(128)} %pad_add_fusion.1.spot_ref, bf16[3136,6272]{1,0:T(8,128)(2,1)} %enlarge.5.rows_ref, bf16[448,6272]{1,0:T(8,128)(2,1)} %get-tuple-element.22.refs_0_), custom_call_target="tpu_custom_call" | custom-call | flops 8811708416 | bytes 19668992 | tf_op jit(solution)/shard_map/project/pallas_call | solution.py:235
  224.8 17.8 %collective-permute-done.22 = bf16[784,448]{1,0:T(8,128)(2,1)S(1)} collective-permute-done((bf16[784,448]{1,0:T(8,128)(2,1)S(1)}, bf16[784,448]{1,0:T(8,128)(2,1)S(1)}, u32[]{:S(2)}, u32[]{:S(2)}) %collective-permute-start.22) | collective-permute-done | bytes 702496 | tf_op jit(solution)/shard_map/ppermute | solution.py:414
  245.1 1.5 collective-permute-done.23
  246.7 1.6 collective-permute-start.24
  251.3 3.2 collective-permute-done.25
  254.5 2.3 collective-permute-start.27
  260.0 4.6 %collective-permute-done.28 = f32[160,128]{1,0:T(8,128)S(1)} collective-permute-done((f32[160,128]{1,0:T(8,128)S(1)}, f32[160,128]{1,0:T(8,128)S(1)}, u32[]{:S(2)}, u32[]{:S(2)}) %collective-permute-start.28) | collective-permute-done | bytes 81952 | tf_op jit(solution)/shard_map/ppermute | solution.py:414
  266.1 2.0 collective-permute-start.32
  271.7 1.6 collective-permute-done.33
  275.5 18.8 %collective-permute-done.34.refs_1_ = bf16[784,448]{1,0:T(8,128)(2,1)S(1)} collective-permute-done((bf16[784,448]{1,0:T(8,128)(2,1)S(1)}, bf16[784,448]{1,0:T(8,128)(2,1)S(1)}, u32[]{:S(2)}, u32[]{:S(2)}) %collective-permute-start.34) | collective-permute-done | bytes 702496 | tf_op jit(solution)/shard_map/ppermute | solution.py:414
  294.9 27.8 %factor.1 = (f32[448,448]{1,0:T(8,128)}, f32[448,448]{1,0:T(8,128)}) custom-call(f32[1280,128]{1,0:T(8,128)} %pad_maximum_fusion.gram_ref), custom_call_target="tpu_custom_call" | custom-call | tf_op jit(solution)/shard_map/factor/pallas_call | solution.py:352
  324.0 6.9 %solve.1 = f32[49,56,112]{2,1,0:T(8,128)} custom-call(s32[4]{0:T(128)} %pad_add_fusion.spots_ref, s32[1]{0:T(128)} %bitcast.own_ref, f32[448,448]{1,0:T(8,128)} %get-tuple-element.27.inverse_ref, bf16[784,448]{1,0:T(8,128)(2,1)} %copy-done, bf16[784,448]{1,0:T(8,128)(2,1)} %copy-done.1, bf16[784,448]{1,0:T(8,128)(2,1)} %copy-done.2, bf16[784,448]{1,0:T(8,128)(2,1)} %copy-done.3), custom_call_target="tpu_custom_call" | custom-call | tf_op jit(solution)/shard_map/solve/pallas_call | solution.py:401
  (118 shorter events, 38.6 us)
Async XLA Ops:
  0.6 22.0 %collective-permute-start.9 = (bf16[49,56,112]{2,1,0:T(8,128)(2,1)}, bf16[49,56,112]{2,1,0:T(8,128)(2,1)S(1)}, u32[]{:S(2)}, u32[]{:S(2)}) collective-permute-start(bf16[49,56,112]{2,1,0:T(8,128)(2,1)} %bitcast.80), channel_id=1, source_target_pairs={{0,24},{1,25},{2,26},{3,27},{4,28},{5,29},{6,30},{7,31},{8,16},{9,... | collective-permute-start | bytes 1843976 | tf_op jit(solution)/shard_map/ppermute | solution.py:414
  5.8 38.8 %collective-permute-start = (bf16[49,56,112]{2,1,0:T(8,128)(2,1)}, bf16[49,56,112]{2,1,0:T(8,128)(2,1)}, u32[]{:S(2)}, u32[]{:S(2)}) collective-permute-start(bf16[49,56,112]{2,1,0:T(8,128)(2,1)} %bitcast.72), channel_id=1, source_target_pairs={{0,2},{1,3},{2,0},{3,1},{4,6},{5,7},{6,4},{7,5},{8,10},{9,11},{10,... | collective-permute-start | bytes 1843976 | tf_op jit(solution)/shard_map/ppermute | solution.py:414
  7.3 37.6 %collective-permute-start.6 = (bf16[49,56,112]{2,1,0:T(8,128)(2,1)}, bf16[49,56,112]{2,1,0:T(8,128)(2,1)}, u32[]{:S(2)}, u32[]{:S(2)}) collective-permute-start(bf16[49,56,112]{2,1,0:T(8,128)(2,1)} %bitcast.81), channel_id=1, source_target_pairs={{0,4},{1,5},{2,6},{3,7},{4,0},{5,1},{6,2},{7,3},{8,12},{9,13},{10,... | collective-permute-start | bytes 1843976 | tf_op jit(solution)/shard_map/ppermute | solution.py:414
  8.8 38.6 %collective-permute-start.7 = (bf16[49,56,112]{2,1,0:T(8,128)(2,1)}, bf16[49,56,112]{2,1,0:T(8,128)(2,1)}, u32[]{:S(2)}, u32[]{:S(2)}) collective-permute-start(bf16[49,56,112]{2,1,0:T(8,128)(2,1)} %bitcast.82), channel_id=1, source_target_pairs={{0,8},{1,9},{2,10},{3,11},{4,12},{5,13},{6,14},{7,15},{8,0},{9,1},... | collective-permute-start | bytes 1843976 | tf_op jit(solution)/shard_map/ppermute | solution.py:414
  22.7 30.0 %collective-permute-start.10 = (bf16[49,56,112]{2,1,0:T(8,128)(2,1)S(1)}, bf16[49,56,112]{2,1,0:T(8,128)(2,1)}, u32[]{:S(2)}, u32[]{:S(2)}) collective-permute-start(bf16[49,56,112]{2,1,0:T(8,128)(2,1)S(1)} %collective-permute-done.9.rest_6_), channel_id=1, source_target_pairs={{0,8},{1,9},{2,10},{3,11},{4,12},{5,13},{6,14},{7,15},{8,0},{9,1},... | collective-permute-start | bytes 1843976 | tf_op jit(solution)/shard_map/ppermute | solution.py:414
  36.5 5.0 %collective-permute-start.3 = (bf16[112,448]{1,0:T(8,128)(2,1)}, bf16[112,448]{1,0:T(8,128)(2,1)S(1)}, u32[]{:S(2)}, u32[]{:S(2)}) collective-permute-start(bf16[112,448]{1,0:T(8,128)(2,1)} %refs_4_.1), channel_id=1, source_target_pairs={{0,2},{1,3},{2,0},{3,1},{4,6},{5,7},{6,4},{7,5},{8,10},{9,11},{10,... | collective-permute-start | bytes 301064 | tf_op jit(solution)/shard_map/ppermute | solution.py:414
  44.4 16.1 %collective-permute-start.1 = (bf16[49,56,112]{2,1,0:T(8,128)(2,1)}, bf16[49,56,112]{2,1,0:T(8,128)(2,1)}, u32[]{:S(2)}, u32[]{:S(2)}) collective-permute-start(bf16[49,56,112]{2,1,0:T(8,128)(2,1)} %bitcast.73), channel_id=1, source_target_pairs={{0,1},{1,0},{2,3},{3,2},{4,5},{5,4},{6,7},{7,6},{8,9},{9,8},{10,11... | collective-permute-start | bytes 1843976 | tf_op jit(solution)/shard_map/ppermute | solution.py:414
  44.6 15.8 %collective-permute-start.2 = (bf16[49,56,112]{2,1,0:T(8,128)(2,1)}, bf16[49,56,112]{2,1,0:T(8,128)(2,1)}, u32[]{:S(2)}, u32[]{:S(2)}) collective-permute-start(bf16[49,56,112]{2,1,0:T(8,128)(2,1)} %collective-permute-done), channel_id=1, source_target_pairs={{0,1},{1,0},{2,3},{3,2},{4,5},{5,4},{6,7},{7,6},{8,9},{9,8},{10,11... | collective-permute-start | bytes 1843976 | tf_op jit(solution)/shard_map/ppermute | solution.py:414
  44.9 25.0 %collective-permute-start.12 = (bf16[49,56,112]{2,1,0:T(8,128)(2,1)}, bf16[49,56,112]{2,1,0:T(8,128)(2,1)}, u32[]{:S(2)}, u32[]{:S(2)}) collective-permute-start(bf16[49,56,112]{2,1,0:T(8,128)(2,1)} %collective-permute-done.6.rest_1_), channel_id=1, source_target_pairs={{0,24},{1,25},{2,26},{3,27},{4,28},{5,29},{6,30},{7,31},{8,16},{9,... | collective-permute-start | bytes 1843976 | tf_op jit(solution)/shard_map/ppermute | solution.py:414
  47.4 22.5 %collective-permute-start.8 = (bf16[49,56,112]{2,1,0:T(8,128)(2,1)}, bf16[49,56,112]{2,1,0:T(8,128)(2,1)}, u32[]{:S(2)}, u32[]{:S(2)}) collective-permute-start(bf16[49,56,112]{2,1,0:T(8,128)(2,1)} %collective-permute-done.7.rest_2_), channel_id=1, source_target_pairs={{0,4},{1,5},{2,6},{3,7},{4,0},{5,1},{6,2},{7,3},{8,12},{9,13},{10,... | collective-permute-start | bytes 1843976 | tf_op jit(solution)/shard_map/ppermute | solution.py:414
  52.6 27.7 %collective-permute-start.11 = (bf16[49,56,112]{2,1,0:T(8,128)(2,1)}, bf16[49,56,112]{2,1,0:T(8,128)(2,1)}, u32[]{:S(2)}, u32[]{:S(2)}) collective-permute-start(bf16[49,56,112]{2,1,0:T(8,128)(2,1)} %collective-permute-done.10.rest_4_), channel_id=1, source_target_pairs={{0,4},{1,5},{2,6},{3,7},{4,0},{5,1},{6,2},{7,3},{8,12},{9,13},{10,... | collective-permute-start | bytes 1843976 | tf_op jit(solution)/shard_map/ppermute | solution.py:414
  80.3 40.4 %collective-permute-start.16 = (bf16[49,56,112]{2,1,0:T(8,128)(2,1)S(1)}, bf16[49,56,112]{2,1,0:T(8,128)(2,1)S(1)}, u32[]{:S(2)}, u32[]{:S(2)}) collective-permute-start(bf16[49,56,112]{2,1,0:T(8,128)(2,1)S(1)} %bitcast.69), channel_id=1, source_target_pairs={{0,24},{1,25},{2,26},{3,27},{4,28},{5,29},{6,30},{7,31},{8,16},{9,... | collective-permute-start | bytes 1843976 | tf_op jit(solution)/shard_map/ppermute | solution.py:414
  81.7 65.4 %collective-permute-start.14 = (bf16[49,56,112]{2,1,0:T(8,128)(2,1)S(1)}, bf16[49,56,112]{2,1,0:T(8,128)(2,1)S(1)}, u32[]{:S(2)}, u32[]{:S(2)}) collective-permute-start(bf16[49,56,112]{2,1,0:T(8,128)(2,1)S(1)} %bitcast.70), channel_id=1, source_target_pairs={{0,8},{1,9},{2,10},{3,11},{4,12},{5,13},{6,14},{7,15},{8,0},{9,1},... | collective-permute-start | bytes 1843976 | tf_op jit(solution)/shard_map/ppermute | solution.py:414
  81.7 66.0 %collective-permute-start.13 = (bf16[49,56,112]{2,1,0:T(8,128)(2,1)S(1)}, bf16[49,56,112]{2,1,0:T(8,128)(2,1)S(1)}, u32[]{:S(2)}, u32[]{:S(2)}) collective-permute-start(bf16[49,56,112]{2,1,0:T(8,128)(2,1)S(1)} %bitcast.71), channel_id=1, source_target_pairs={{0,4},{1,5},{2,6},{3,7},{4,0},{5,1},{6,2},{7,3},{8,12},{9,13},{10,... | collective-permute-start | bytes 1843976 | tf_op jit(solution)/shard_map/ppermute | solution.py:414
  120.8 29.4 %collective-permute-start.17 = (bf16[49,56,112]{2,1,0:T(8,128)(2,1)S(1)}, bf16[49,56,112]{2,1,0:T(8,128)(2,1)S(1)}, u32[]{:S(2)}, u32[]{:S(2)}) collective-permute-start(bf16[49,56,112]{2,1,0:T(8,128)(2,1)S(1)} %collective-permute-done.16.refs_6_), channel_id=1, source_target_pairs={{0,8},{1,9},{2,10},{3,11},{4,12},{5,13},{6,14},{7,15},{8,0},{9,1},... | collective-permute-start | bytes 1843976 | tf_op jit(solution)/shard_map/ppermute | solution.py:414
  147.1 28.9 %collective-permute-start.15 = (bf16[49,56,112]{2,1,0:T(8,128)(2,1)S(1)}, bf16[49,56,112]{2,1,0:T(8,128)(2,1)}, u32[]{:S(2)}, u32[]{:S(2)}) collective-permute-start(bf16[49,56,112]{2,1,0:T(8,128)(2,1)S(1)} %collective-permute-done.14.refs_2_), channel_id=1, source_target_pairs={{0,4},{1,5},{2,6},{3,7},{4,0},{5,1},{6,2},{7,3},{8,12},{9,13},{10,... | collective-permute-start | bytes 1843976 | tf_op jit(solution)/shard_map/ppermute | solution.py:414
  147.7 28.3 %collective-permute-start.19 = (bf16[49,56,112]{2,1,0:T(8,128)(2,1)S(1)}, bf16[49,56,112]{2,1,0:T(8,128)(2,1)S(1)}, u32[]{:S(2)}, u32[]{:S(2)}) collective-permute-start(bf16[49,56,112]{2,1,0:T(8,128)(2,1)S(1)} %collective-permute-done.13.refs_1_), channel_id=1, source_target_pairs={{0,24},{1,25},{2,26},{3,27},{4,28},{5,29},{6,30},{7,31},{8,16},{9,... | collective-permute-start | bytes 1843976 | tf_op jit(solution)/shard_map/ppermute | solution.py:414
  150.2 27.7 %collective-permute-start.18 = (bf16[49,56,112]{2,1,0:T(8,128)(2,1)S(1)}, bf16[49,56,112]{2,1,0:T(8,128)(2,1)S(1)}, u32[]{:S(2)}, u32[]{:S(2)}) collective-permute-start(bf16[49,56,112]{2,1,0:T(8,128)(2,1)S(1)} %collective-permute-done.17.refs_4_), channel_id=1, source_target_pairs={{0,4},{1,5},{2,6},{3,7},{4,0},{5,1},{6,2},{7,3},{8,12},{9,13},{10,... | collective-permute-start | bytes 1843976 | tf_op jit(solution)/shard_map/ppermute | solution.py:414
  200.6 2.6 collective-permute-start.20
  222.4 20.2 %collective-permute-start.22 = (bf16[784,448]{1,0:T(8,128)(2,1)S(1)}, bf16[784,448]{1,0:T(8,128)(2,1)S(1)}, u32[]{:S(2)}, u32[]{:S(2)}) collective-permute-start(bf16[784,448]{1,0:T(8,128)(2,1)S(1)} %add_convert_fusion.1), channel_id=1, source_target_pairs={{0,2},{1,3},{2,0},{3,1},{4,6},{5,7},{6,4},{7,5},{8,10},{9,11},{10,... | collective-permute-start | bytes 2107400 | tf_op jit(solution)/shard_map/ppermute | solution.py:414
  246.7 4.6 %collective-permute-start.24 = (f32[160,128]{1,0:T(8,128)S(1)}, f32[160,128]{1,0:T(8,128)S(1)}, u32[]{:S(2)}, u32[]{:S(2)}) collective-permute-start(f32[160,128]{1,0:T(8,128)S(1)} %get-tuple-element.38), channel_id=1, source_target_pairs={{0,2},{1,3},{2,0},{3,1},{4,6},{5,7},{6,4},{7,5},{8,10},{9,11},{10,... | collective-permute-start | bytes 245768 | tf_op jit(solution)/shard_map/ppermute | solution.py:414
  248.3 6.2 %collective-permute-start.25 = (f32[160,128]{1,0:T(8,128)S(1)}, f32[160,128]{1,0:T(8,128)S(1)}, u32[]{:S(2)}, u32[]{:S(2)}) collective-permute-start(f32[160,128]{1,0:T(8,128)S(1)} %get-tuple-element.40), channel_id=1, source_target_pairs={{0,4},{1,5},{2,6},{3,7},{4,0},{5,1},{6,2},{7,3},{8,12},{9,13},{10,... | collective-permute-start | bytes 245768 | tf_op jit(solution)/shard_map/ppermute | solution.py:414
  248.8 5.7 %collective-permute-start.26 = (f32[160,128]{1,0:T(8,128)S(1)}, f32[160,128]{1,0:T(8,128)S(1)}, u32[]{:S(2)}, u32[]{:S(2)}) collective-permute-start(f32[160,128]{1,0:T(8,128)S(1)} %get-tuple-element.39), channel_id=1, source_target_pairs={{0,6},{1,7},{2,4},{3,5},{4,2},{5,3},{6,0},{7,1},{8,14},{9,15},{10,... | collective-permute-start | bytes 245768 | tf_op jit(solution)/shard_map/ppermute | solution.py:414
  254.5 5.5 %collective-permute-start.27 = (f32[160,128]{1,0:T(8,128)S(1)}, f32[160,128]{1,0:T(8,128)S(1)}, u32[]{:S(2)}, u32[]{:S(2)}) collective-permute-start(f32[160,128]{1,0:T(8,128)S(1)} %fusion.6), channel_id=1, source_target_pairs={{0,8},{1,9},{2,10},{3,11},{4,12},{5,13},{6,14},{7,15},{8,0},{9,1},... | collective-permute-start | bytes 245768 | tf_op jit(solution)/shard_map/ppermute | solution.py:414
  256.8 7.8 %collective-permute-start.28 = (f32[160,128]{1,0:T(8,128)S(1)}, f32[160,128]{1,0:T(8,128)S(1)}, u32[]{:S(2)}, u32[]{:S(2)}) collective-permute-start(f32[160,128]{1,0:T(8,128)S(1)} %fusion.6), channel_id=1, source_target_pairs={{0,16},{1,17},{2,18},{3,19},{4,20},{5,21},{6,22},{7,23},{8,24},{9,... | collective-permute-start | bytes 245768 | tf_op jit(solution)/shard_map/ppermute | solution.py:414
  257.9 6.7 %collective-permute-start.29 = (f32[160,128]{1,0:T(8,128)S(1)}, f32[160,128]{1,0:T(8,128)S(1)}, u32[]{:S(2)}, u32[]{:S(2)}) collective-permute-start(f32[160,128]{1,0:T(8,128)S(1)} %fusion.6), channel_id=1, source_target_pairs={{0,24},{1,25},{2,26},{3,27},{4,28},{5,29},{6,30},{7,31},{8,16},{9,... | collective-permute-start | bytes 245768 | tf_op jit(solution)/shard_map/ppermute | solution.py:414
  264.6 4.5 %collective-permute-start.30 = (f32[160,128]{1,0:T(8,128)S(1)}, f32[160,128]{1,0:T(8,128)S(1)}, u32[]{:S(2)}, u32[]{:S(2)}) collective-permute-start(f32[160,128]{1,0:T(8,128)S(1)} %add_add_fusion), channel_id=1, source_target_pairs={{0,2},{1,3},{2,0},{3,1},{4,6},{5,7},{6,4},{7,5},{8,10},{9,11},{10,... | collective-permute-start | bytes 245768 | tf_op jit(solution)/shard_map/ppermute | solution.py:414
  265.5 4.4 %collective-permute-start.31 = (f32[160,128]{1,0:T(8,128)S(1)}, f32[160,128]{1,0:T(8,128)S(1)}, u32[]{:S(2)}, u32[]{:S(2)}) collective-permute-start(f32[160,128]{1,0:T(8,128)S(1)} %add_add_fusion), channel_id=1, source_target_pairs={{0,4},{1,5},{2,6},{3,7},{4,0},{5,1},{6,2},{7,3},{8,12},{9,13},{10,... | collective-permute-start | bytes 245768 | tf_op jit(solution)/shard_map/ppermute | solution.py:414
  266.1 5.3 %collective-permute-start.32 = (f32[160,128]{1,0:T(8,128)S(1)}, f32[160,128]{1,0:T(8,128)S(1)}, u32[]{:S(2)}, u32[]{:S(2)}) collective-permute-start(f32[160,128]{1,0:T(8,128)S(1)} %add_add_fusion), channel_id=1, source_target_pairs={{0,6},{1,7},{2,4},{3,5},{4,2},{5,3},{6,0},{7,1},{8,14},{9,15},{10,... | collective-permute-start | bytes 245768 | tf_op jit(solution)/shard_map/ppermute | solution.py:414
  274.3 19.9 %collective-permute-start.34 = (bf16[784,448]{1,0:T(8,128)(2,1)S(1)}, bf16[784,448]{1,0:T(8,128)(2,1)S(1)}, u32[]{:S(2)}, u32[]{:S(2)}) collective-permute-start(bf16[784,448]{1,0:T(8,128)(2,1)S(1)} %add_convert_fusion.refs_0_), channel_id=1, source_target_pairs={{0,2},{1,3},{2,0},{3,1},{4,6},{5,7},{6,4},{7,5},{8,10},{9,11},{10,... | collective-permute-start | bytes 2107400 | tf_op jit(solution)/shard_map/ppermute | solution.py:414
  275.5 47.3 %collective-permute-start.35 = (bf16[784,448]{1,0:T(8,128)(2,1)S(1)}, bf16[784,448]{1,0:T(8,128)(2,1)S(1)}, u32[]{:S(2)}, u32[]{:S(2)}) collective-permute-start(bf16[784,448]{1,0:T(8,128)(2,1)S(1)} %add_convert_fusion.refs_0_), channel_id=1, source_target_pairs={{0,1},{1,0},{2,3},{3,2},{4,5},{5,4},{6,7},{7,6},{8,9},{9,8},{10,11... | collective-permute-start | bytes 2107400 | tf_op jit(solution)/shard_map/ppermute | solution.py:414
  294.2 28.6 %collective-permute-start.36 = (bf16[784,448]{1,0:T(8,128)(2,1)S(1)}, bf16[784,448]{1,0:T(8,128)(2,1)S(1)}, u32[]{:S(2)}, u32[]{:S(2)}) collective-permute-start(bf16[784,448]{1,0:T(8,128)(2,1)S(1)} %collective-permute-done.34.refs_1_), channel_id=1, source_target_pairs={{0,1},{1,0},{2,3},{3,2},{4,5},{5,4},{6,7},{7,6},{8,9},{9,8},{10,11... | collective-permute-start | bytes 2107400 | tf_op jit(solution)/shard_map/ppermute | solution.py:414
  (20 other events, 277.9 us)

commit v3 on v2

--- a/solution.py
+++ b/solution.py
@@ -254,10 +254,16 @@
         unit = (lane == row + k * BLOCK).astype(F32)
         work[k, :, :size] = jnp.where(lane >= real, unit, 0.0)
         work[k, :, size:] = unit
-        for j in range(k, blocks):
+        narrow = paired(real)
+        for j in range(k, blocks - narrow):
             at = slice(j * BLOCK, (j + 1) * BLOCK)
             work[k, :, at] = work[k, :, at] + gram_ref[place * BLOCK:(place + 1) * BLOCK, :]
             place += 1
+    if paired(real):
+        half = BLOCK // 2
+        for k in range(blocks):
+            data = gram_ref[(place + k // 2) * BLOCK:(place + k // 2 + 1) * BLOCK, :]
+            work[k, :, size - BLOCK:size - half] = data[:, k % 2 * half:(k % 2 + 1) * half]
     sub = lax.broadcasted_iota(jnp.int32, (PANEL, BLOCK), 0)
     lane8 = lax.broadcasted_iota(jnp.int32, (PANEL, BLOCK), 1)
     panels = BLOCK // PANEL
@@ -337,13 +343,22 @@
         inverse_ref[at, :] = work[k, :count, size:size + real]
 
 
+def paired(real):
+    return real % BLOCK == BLOCK // 2 and -(-real // BLOCK) % 2 == 0
+
+
 def packed_blocks(gram):
     real = gram.shape[0]
     spare = -real % BLOCK
     gram = jnp.pad(gram, ((0, spare), (0, spare)))
     blocks = gram.shape[0] // BLOCK
-    return jnp.concatenate([gram[i * BLOCK:(i + 1) * BLOCK, j * BLOCK:(j + 1) * BLOCK]
-                            for i in range(blocks) for j in range(i, blocks)])
+    narrow = paired(real)
+    block = lambda i, j, width: gram[i * BLOCK:(i + 1) * BLOCK, j * BLOCK:j * BLOCK + width]
+    whole = [block(i, j, BLOCK) for i in range(blocks) for j in range(i, blocks - narrow)]
+    if narrow:
+        whole += [jnp.concatenate([block(i + n, blocks - 1, BLOCK // 2) for n in range(2)], axis=1)
+                  for i in range(0, blocks, 2)]
+    return jnp.concatenate(whole)
 
 
 def factorize(packed, real):

time: 332 us -> 332 us (level)
  transfers between devices with their start and end apart: 37 -> 37, of which waited for: 20 -> 22; matrix products, arithmetic and copies ran while one was open for 3% -> 3% of each run, Pallas kernels for 37% -> 37%
where the time goes in v3:
time: 332 us; the launch traced here: 331 us
  Pallas kernels  170 us (51%)
  waiting for transfers between devices  87.6 us (26%)
  starting transfers between devices  54.7 us (16%)
  local copies, waits for them, and re-layouts  9.25 us (3%)
  other arithmetic  7.52 us (2%)
    ppermute x37, waiting for transfers between devices, swap(): lax.ppermute(x, ('wide', 'narrow'), [(i, i ^ mask) for i in range(count)])  87.6 us
    pallas_call x3, Pallas kernels, enlarge(): pl.pallas_call(functools.partial(enlarge_kernel, layout_of(pieces) if pie...  86 us
    ppermute x37, starting transfers between devices, swap(): lax.ppermute(x, ('wide', 'narrow'), [(i, i ^ mask) for i in range(count)])  54.7 us
    pallas_call x2, Pallas kernels, project(): pl.pallas_call(functools.partial(project_kernel, layout_of(pieces) if pie...  39.6 us
    pallas_call x1, Pallas kernels, factorize(): pl.pallas_call(functools.partial(factor_kernel, real), out_shape=(jax.Sha...  27.8 us
    pallas_call x1, Pallas kernels, half_left_of(): pl.pallas_call(functools.partial(half_left_kernel, len(lefts)), out_shape...  9.44 us
    pallas_call x1, Pallas kernels, solve(): pl.pallas_call(functools.partial(solve_kernel, len(pieces)), in_specs=[sm...  6.93 us
  transfers between devices with their start and end apart: 37, of which 22 were waited for; matrix products, arithmetic and copies ran while one was open for 3% of the time, Pallas kernels for 37%

profile of v3, /device:TPU:0, one launch (start us, length us, event | category | flops | bytes accessed | tf_op | source)
XLA Modules:
  0.0 330.8 jit_solution(6296859890022541919)
XLA Ops:
  0.6 5.1 %collective-permute-start.9 = (bf16[49,56,112]{2,1,0:T(8,128)(2,1)}, bf16[49,56,112]{2,1,0:T(8,128)(2,1)S(1)}, u32[]{:S(2)}, u32[]{:S(2)}) collective-permute-start(bf16[49,56,112]{2,1,0:T(8,128)(2,1)} %bitcast.79), channel_id=1, source_target_pairs={{0,24},{1,25},{2,26},{3,27},{4,28},{5,29},{6,30},{7,31},{8,16},{9,... | collective-permute-start | bytes 1843976 | tf_op jit(solution)/shard_map/ppermute | solution.py:429
  7.3 1.5 collective-permute-start.6
  8.8 13.9 %collective-permute-done.9.rest_6_ = bf16[49,56,112]{2,1,0:T(8,128)(2,1)S(1)} collective-permute-done((bf16[49,56,112]{2,1,0:T(8,128)(2,1)}, bf16[49,56,112]{2,1,0:T(8,128)(2,1)S(1)}, u32[]{:S(2)}, u32[]{:S(2)}) %collective-permute-start.9) | collective-permute-done | bytes 614688 | tf_op jit(solution)/shard_map/ppermute | solution.py:429
  22.7 13.8 %collective-permute-start.10 = (bf16[49,56,112]{2,1,0:T(8,128)(2,1)S(1)}, bf16[49,56,112]{2,1,0:T(8,128)(2,1)}, u32[]{:S(2)}, u32[]{:S(2)}) collective-permute-start(bf16[49,56,112]{2,1,0:T(8,128)(2,1)S(1)} %collective-permute-done.9.rest_6_), channel_id=1, source_target_pairs={{0,8},{1,9},{2,10},{3,11},{4,12},{5,13},{6,14},{7,15},{8,0},{9,1},... | collective-permute-start | bytes 1843976 | tf_op jit(solution)/shard_map/ppermute | solution.py:429
  38.0 3.5 %collective-permute-done.3.refs_5_ = bf16[112,448]{1,0:T(8,128)(2,1)S(1)} collective-permute-done((bf16[112,448]{1,0:T(8,128)(2,1)}, bf16[112,448]{1,0:T(8,128)(2,1)S(1)}, u32[]{:S(2)}, u32[]{:S(2)}) %collective-permute-start.3) | collective-permute-done | bytes 100384 | tf_op jit(solution)/shard_map/ppermute | solution.py:429
  44.9 2.5 collective-permute-start.12
  47.4 1.5 collective-permute-start.8
  48.9 3.7 %collective-permute-done.10.rest_4_ = bf16[49,56,112]{2,1,0:T(8,128)(2,1)} collective-permute-done((bf16[49,56,112]{2,1,0:T(8,128)(2,1)S(1)}, bf16[49,56,112]{2,1,0:T(8,128)(2,1)}, u32[]{:S(2)}, u32[]{:S(2)}) %collective-permute-start.10) | collective-permute-done | bytes 614688 | tf_op jit(solution)/shard_map/ppermute | solution.py:429
  52.6 1.5 collective-permute-start.11
  55.3 2.2 mul.24.first_ref
  60.4 9.4 %half_left.1.half_ref = bf16[3136,448]{1,0:T(8,128)(2,1)} custom-call(bf16[2744,112]{1,0:T(8,128)(2,1)} %bitcast.72, bf16[2744,112]{1,0:T(8,128)(2,1)} %bitcast.8.refs_1_, bf16[2744,112]{1,0:T(8,128)(2,1)} %bitcast.9.refs_2_, bf16[2744,112]{1,0:T(8,128)(2,1)} %bitcast.10.refs_3_, bf16[112,448]{1,0:T(8,128)(2,1)} %refs_4_.1, bf16[112,448]{1,0:T(8,128)(2,1)} %copy-done.11, ...), custom_call_target="tpu_custom_call" | custom-call | tf_op jit(solution)/shard_map/half_left/pallas_call | solution.py:91
  69.9 10.5 %collective-permute-done.11.rest_5_ = bf16[49,56,112]{2,1,0:T(8,128)(2,1)} collective-permute-done((bf16[49,56,112]{2,1,0:T(8,128)(2,1)}, bf16[49,56,112]{2,1,0:T(8,128)(2,1)}, u32[]{:S(2)}, u32[]{:S(2)}) %collective-permute-start.11) | collective-permute-done | bytes 614688 | tf_op jit(solution)/shard_map/ppermute | solution.py:429
  83.2 37.5 %enlarge.3 = (bf16[3136,6272]{1,0:T(8,128)(2,1)}, bf16[448,6272]{1,0:T(8,128)(2,1)}) custom-call(s32[8]{0:T(128)} %iota_xor_fusion.order_ref, bf16[3136,448]{1,0:T(8,128)(2,1)} %half_left.1.half_ref, bf16[392,224]{1,0:T(8,128)(2,1)} %mul.24.first_ref, bf16[56,112]{1,0:T(8,128)(2,1)} %copy.15.second_ref, bf16[49,56,112]{2,1,0:T(8,128)(2,1)} %bitcast.82, ...), custom_call_target="tpu_custom_call" | custom-call | flops 19730006016 | bytes 16859136 | tf_op jit(solution)/shard_map/enlarge/pallas_call | solution.py:185
  120.8 2.1 collective-permute-start.17
  122.8 24.3 %enlarge.4.rest_1_ = bf16[3136,6272]{1,0:T(8,128)(2,1)} custom-call(s32[8]{0:T(128)} %iota_xor_fusion.order_ref, bf16[3136,448]{1,0:T(8,128)(2,1)} %half_left.1.half_ref, bf16[392,224]{1,0:T(8,128)(2,1)} %mul.24.first_ref, bf16[56,112]{1,0:T(8,128)(2,1)} %copy.15.second_ref, ...), custom_call_target="tpu_custom_call", output_to_operand_aliasing={{}: (5, {})} | custom-call | flops 13153337344 | bytes 11239424 | tf_op jit(solution)/shard_map/enlarge/pallas_call | solution.py:185
  147.7 2.5 collective-permute-start.19
  151.7 24.3 %enlarge.5.rows_ref = bf16[3136,6272]{1,0:T(8,128)(2,1)} custom-call(s32[8]{0:T(128)} %iota_xor_fusion.order_ref, bf16[3136,448]{1,0:T(8,128)(2,1)} %half_left.1.half_ref, bf16[392,224]{1,0:T(8,128)(2,1)} %mul.24.first_ref, bf16[56,112]{1,0:T(8,128)(2,1)} %copy.15.second_ref, ...), custom_call_target="tpu_custom_call", output_to_operand_aliasing={{}: (5, {})} | custom-call | flops 13153337344 | bytes 11239424 | tf_op jit(solution)/shard_map/enlarge/pallas_call | solution.py:185
  176.0 1.9 collective-permute-done.18.refs_5_
  178.7 21.8 %project.2 = (bf16[784,448]{1,0:T(8,128)(2,1)}, bf16[784,448]{1,0:T(8,128)(2,1)}, bf16[448,6272]{1,0:T(8,128)(2,1)}) custom-call(s32[8]{0:T(128)} %iota_xor_fusion.order_ref, s32[2]{0:T(128)} %pad_add_fusion.2.spot_ref, bf16[3136,6272]{1,0:T(8,128)(2,1)} %enlarge.5.rows_ref, bf16[49,56,112]{2,1,0:T(8,128)(2,1)} %bitcast.66, bf16[49,56,112]{2,1,0:T(8,128)(2,1)} %copy-done.7, ...), custom_call_target="tpu_custom_call" | custom-call | flops 8811708416 | bytes 19668992 | tf_op jit(solution)/shard_map/project/pallas_call | solution.py:235
  201.3 1.9 collective-permute-done.20
  204.5 17.7 %project.3 = (bf16[784,448]{1,0:T(8,128)(2,1)}, bf16[784,448]{1,0:T(8,128)(2,1)}) custom-call(s32[8]{0:T(128)} %iota_xor_fusion.order_ref, s32[2]{0:T(128)} %pad_add_fusion.1.spot_ref, bf16[3136,6272]{1,0:T(8,128)(2,1)} %enlarge.5.rows_ref, bf16[448,6272]{1,0:T(8,128)(2,1)} %get-tuple-element.22.refs_0_), custom_call_target="tpu_custom_call" | custom-call | flops 8811708416 | bytes 19668992 | tf_op jit(solution)/shard_map/project/pallas_call | solution.py:235
  224.8 17.8 %collective-permute-done.22 = bf16[784,448]{1,0:T(8,128)(2,1)S(1)} collective-permute-done((bf16[784,448]{1,0:T(8,128)(2,1)S(1)}, bf16[784,448]{1,0:T(8,128)(2,1)S(1)}, u32[]{:S(2)}, u32[]{:S(2)}) %collective-permute-start.22) | collective-permute-done | bytes 702496 | tf_op jit(solution)/shard_map/ppermute | solution.py:429
  247.6 1.6 collective-permute-start.24
  251.9 2.2 collective-permute-done.25
  254.9 2.6 collective-permute-start.27
  260.4 3.1 collective-permute-done.28
  266.2 2.1 collective-permute-start.32
  269.6 1.7 collective-permute-done.32
  271.5 1.5 collective-permute-done.33
  275.5 18.5 %collective-permute-done.34.refs_1_ = bf16[784,448]{1,0:T(8,128)(2,1)S(1)} collective-permute-done((bf16[784,448]{1,0:T(8,128)(2,1)S(1)}, bf16[784,448]{1,0:T(8,128)(2,1)S(1)}, u32[]{:S(2)}, u32[]{:S(2)}) %collective-permute-start.34) | collective-permute-done | bytes 702496 | tf_op jit(solution)/shard_map/ppermute | solution.py:429
  294.7 27.8 %factor.1 = (f32[448,448]{1,0:T(8,128)}, f32[448,448]{1,0:T(8,128)}) custom-call(f32[1024,128]{1,0:T(8,128)} %pad_maximum_fusion.gram_ref), custom_call_target="tpu_custom_call" | custom-call | tf_op jit(solution)/shard_map/factor/pallas_call | solution.py:367
  323.7 6.9 %solve.1 = f32[49,56,112]{2,1,0:T(8,128)} custom-call(s32[4]{0:T(128)} %pad_add_fusion.spots_ref, s32[1]{0:T(128)} %bitcast.own_ref, f32[448,448]{1,0:T(8,128)} %get-tuple-element.27.inverse_ref, bf16[784,448]{1,0:T(8,128)(2,1)} %copy-done, bf16[784,448]{1,0:T(8,128)(2,1)} %copy-done.1, bf16[784,448]{1,0:T(8,128)(2,1)} %copy-done.2, bf16[784,448]{1,0:T(8,128)(2,1)} %copy-done.3), custom_call_target="tpu_custom_call" | custom-call | tf_op jit(solution)/shard_map/solve/pallas_call | solution.py:416
  (120 shorter events, 40.6 us)
Async XLA Ops:
  0.6 22.0 %collective-permute-start.9 = (bf16[49,56,112]{2,1,0:T(8,128)(2,1)}, bf16[49,56,112]{2,1,0:T(8,128)(2,1)S(1)}, u32[]{:S(2)}, u32[]{:S(2)}) collective-permute-start(bf16[49,56,112]{2,1,0:T(8,128)(2,1)} %bitcast.79), channel_id=1, source_target_pairs={{0,24},{1,25},{2,26},{3,27},{4,28},{5,29},{6,30},{7,31},{8,16},{9,... | collective-permute-start | bytes 1843976 | tf_op jit(solution)/shard_map/ppermute | solution.py:429
  5.8 38.8 %collective-permute-start = (bf16[49,56,112]{2,1,0:T(8,128)(2,1)}, bf16[49,56,112]{2,1,0:T(8,128)(2,1)}, u32[]{:S(2)}, u32[]{:S(2)}) collective-permute-start(bf16[49,56,112]{2,1,0:T(8,128)(2,1)} %bitcast.70), channel_id=1, source_target_pairs={{0,2},{1,3},{2,0},{3,1},{4,6},{5,7},{6,4},{7,5},{8,10},{9,11},{10,... | collective-permute-start | bytes 1843976 | tf_op jit(solution)/shard_map/ppermute | solution.py:429
  7.3 37.6 %collective-permute-start.6 = (bf16[49,56,112]{2,1,0:T(8,128)(2,1)}, bf16[49,56,112]{2,1,0:T(8,128)(2,1)}, u32[]{:S(2)}, u32[]{:S(2)}) collective-permute-start(bf16[49,56,112]{2,1,0:T(8,128)(2,1)} %bitcast.80), channel_id=1, source_target_pairs={{0,4},{1,5},{2,6},{3,7},{4,0},{5,1},{6,2},{7,3},{8,12},{9,13},{10,... | collective-permute-start | bytes 1843976 | tf_op jit(solution)/shard_map/ppermute | solution.py:429
  8.8 38.6 %collective-permute-start.7 = (bf16[49,56,112]{2,1,0:T(8,128)(2,1)}, bf16[49,56,112]{2,1,0:T(8,128)(2,1)}, u32[]{:S(2)}, u32[]{:S(2)}) collective-permute-start(bf16[49,56,112]{2,1,0:T(8,128)(2,1)} %bitcast.81), channel_id=1, source_target_pairs={{0,8},{1,9},{2,10},{3,11},{4,12},{5,13},{6,14},{7,15},{8,0},{9,1},... | collective-permute-start | bytes 1843976 | tf_op jit(solution)/shard_map/ppermute | solution.py:429
  22.7 30.0 %collective-permute-start.10 = (bf16[49,56,112]{2,1,0:T(8,128)(2,1)S(1)}, bf16[49,56,112]{2,1,0:T(8,128)(2,1)}, u32[]{:S(2)}, u32[]{:S(2)}) collective-permute-start(bf16[49,56,112]{2,1,0:T(8,128)(2,1)S(1)} %collective-permute-done.9.rest_6_), channel_id=1, source_target_pairs={{0,8},{1,9},{2,10},{3,11},{4,12},{5,13},{6,14},{7,15},{8,0},{9,1},... | collective-permute-start | bytes 1843976 | tf_op jit(solution)/shard_map/ppermute | solution.py:429
  36.5 5.0 %collective-permute-start.3 = (bf16[112,448]{1,0:T(8,128)(2,1)}, bf16[112,448]{1,0:T(8,128)(2,1)S(1)}, u32[]{:S(2)}, u32[]{:S(2)}) collective-permute-start(bf16[112,448]{1,0:T(8,128)(2,1)} %refs_4_.1), channel_id=1, source_target_pairs={{0,2},{1,3},{2,0},{3,1},{4,6},{5,7},{6,4},{7,5},{8,10},{9,11},{10,... | collective-permute-start | bytes 301064 | tf_op jit(solution)/shard_map/ppermute | solution.py:429
  44.4 16.1 %collective-permute-start.1 = (bf16[49,56,112]{2,1,0:T(8,128)(2,1)}, bf16[49,56,112]{2,1,0:T(8,128)(2,1)}, u32[]{:S(2)}, u32[]{:S(2)}) collective-permute-start(bf16[49,56,112]{2,1,0:T(8,128)(2,1)} %bitcast.71), channel_id=1, source_target_pairs={{0,1},{1,0},{2,3},{3,2},{4,5},{5,4},{6,7},{7,6},{8,9},{9,8},{10,11... | collective-permute-start | bytes 1843976 | tf_op jit(solution)/shard_map/ppermute | solution.py:429
  44.6 15.8 %collective-permute-start.2 = (bf16[49,56,112]{2,1,0:T(8,128)(2,1)}, bf16[49,56,112]{2,1,0:T(8,128)(2,1)}, u32[]{:S(2)}, u32[]{:S(2)}) collective-permute-start(bf16[49,56,112]{2,1,0:T(8,128)(2,1)} %collective-permute-done), channel_id=1, source_target_pairs={{0,1},{1,0},{2,3},{3,2},{4,5},{5,4},{6,7},{7,6},{8,9},{9,8},{10,11... | collective-permute-start | bytes 1843976 | tf_op jit(solution)/shard_map/ppermute | solution.py:429
  44.9 25.0 %collective-permute-start.12 = (bf16[49,56,112]{2,1,0:T(8,128)(2,1)}, bf16[49,56,112]{2,1,0:T(8,128)(2,1)}, u32[]{:S(2)}, u32[]{:S(2)}) collective-permute-start(bf16[49,56,112]{2,1,0:T(8,128)(2,1)} %collective-permute-done.6.rest_1_), channel_id=1, source_target_pairs={{0,24},{1,25},{2,26},{3,27},{4,28},{5,29},{6,30},{7,31},{8,16},{9,... | collective-permute-start | bytes 1843976 | tf_op jit(solution)/shard_map/ppermute | solution.py:429
  47.4 22.5 %collective-permute-start.8 = (bf16[49,56,112]{2,1,0:T(8,128)(2,1)}, bf16[49,56,112]{2,1,0:T(8,128)(2,1)}, u32[]{:S(2)}, u32[]{:S(2)}) collective-permute-start(bf16[49,56,112]{2,1,0:T(8,128)(2,1)} %collective-permute-done.7.rest_2_), channel_id=1, source_target_pairs={{0,4},{1,5},{2,6},{3,7},{4,0},{5,1},{6,2},{7,3},{8,12},{9,13},{10,... | collective-permute-start | bytes 1843976 | tf_op jit(solution)/shard_map/ppermute | solution.py:429
  52.6 27.7 %collective-permute-start.11 = (bf16[49,56,112]{2,1,0:T(8,128)(2,1)}, bf16[49,56,112]{2,1,0:T(8,128)(2,1)}, u32[]{:S(2)}, u32[]{:S(2)}) collective-permute-start(bf16[49,56,112]{2,1,0:T(8,128)(2,1)} %collective-permute-done.10.rest_4_), channel_id=1, source_target_pairs={{0,4},{1,5},{2,6},{3,7},{4,0},{5,1},{6,2},{7,3},{8,12},{9,13},{10,... | collective-permute-start | bytes 1843976 | tf_op jit(solution)/shard_map/ppermute | solution.py:429
  80.3 40.4 %collective-permute-start.16 = (bf16[49,56,112]{2,1,0:T(8,128)(2,1)S(1)}, bf16[49,56,112]{2,1,0:T(8,128)(2,1)S(1)}, u32[]{:S(2)}, u32[]{:S(2)}) collective-permute-start(bf16[49,56,112]{2,1,0:T(8,128)(2,1)S(1)} %bitcast.67), channel_id=1, source_target_pairs={{0,24},{1,25},{2,26},{3,27},{4,28},{5,29},{6,30},{7,31},{8,16},{9,... | collective-permute-start | bytes 1843976 | tf_op jit(solution)/shard_map/ppermute | solution.py:429
  81.7 65.4 %collective-permute-start.14 = (bf16[49,56,112]{2,1,0:T(8,128)(2,1)S(1)}, bf16[49,56,112]{2,1,0:T(8,128)(2,1)S(1)}, u32[]{:S(2)}, u32[]{:S(2)}) collective-permute-start(bf16[49,56,112]{2,1,0:T(8,128)(2,1)S(1)} %bitcast.68), channel_id=1, source_target_pairs={{0,8},{1,9},{2,10},{3,11},{4,12},{5,13},{6,14},{7,15},{8,0},{9,1},... | collective-permute-start | bytes 1843976 | tf_op jit(solution)/shard_map/ppermute | solution.py:429
  81.7 66.0 %collective-permute-start.13 = (bf16[49,56,112]{2,1,0:T(8,128)(2,1)S(1)}, bf16[49,56,112]{2,1,0:T(8,128)(2,1)S(1)}, u32[]{:S(2)}, u32[]{:S(2)}) collective-permute-start(bf16[49,56,112]{2,1,0:T(8,128)(2,1)S(1)} %bitcast.69), channel_id=1, source_target_pairs={{0,4},{1,5},{2,6},{3,7},{4,0},{5,1},{6,2},{7,3},{8,12},{9,13},{10,... | collective-permute-start | bytes 1843976 | tf_op jit(solution)/shard_map/ppermute | solution.py:429
  120.8 29.4 %collective-permute-start.17 = (bf16[49,56,112]{2,1,0:T(8,128)(2,1)S(1)}, bf16[49,56,112]{2,1,0:T(8,128)(2,1)S(1)}, u32[]{:S(2)}, u32[]{:S(2)}) collective-permute-start(bf16[49,56,112]{2,1,0:T(8,128)(2,1)S(1)} %collective-permute-done.16.refs_6_), channel_id=1, source_target_pairs={{0,8},{1,9},{2,10},{3,11},{4,12},{5,13},{6,14},{7,15},{8,0},{9,1},... | collective-permute-start | bytes 1843976 | tf_op jit(solution)/shard_map/ppermute | solution.py:429
  147.1 28.9 %collective-permute-start.15 = (bf16[49,56,112]{2,1,0:T(8,128)(2,1)S(1)}, bf16[49,56,112]{2,1,0:T(8,128)(2,1)}, u32[]{:S(2)}, u32[]{:S(2)}) collective-permute-start(bf16[49,56,112]{2,1,0:T(8,128)(2,1)S(1)} %collective-permute-done.14.refs_2_), channel_id=1, source_target_pairs={{0,4},{1,5},{2,6},{3,7},{4,0},{5,1},{6,2},{7,3},{8,12},{9,13},{10,... | collective-permute-start | bytes 1843976 | tf_op jit(solution)/shard_map/ppermute | solution.py:429
  147.7 28.3 %collective-permute-start.19 = (bf16[49,56,112]{2,1,0:T(8,128)(2,1)S(1)}, bf16[49,56,112]{2,1,0:T(8,128)(2,1)S(1)}, u32[]{:S(2)}, u32[]{:S(2)}) collective-permute-start(bf16[49,56,112]{2,1,0:T(8,128)(2,1)S(1)} %collective-permute-done.13.refs_1_), channel_id=1, source_target_pairs={{0,24},{1,25},{2,26},{3,27},{4,28},{5,29},{6,30},{7,31},{8,16},{9,... | collective-permute-start | bytes 1843976 | tf_op jit(solution)/shard_map/ppermute | solution.py:429
  150.2 27.7 %collective-permute-start.18 = (bf16[49,56,112]{2,1,0:T(8,128)(2,1)S(1)}, bf16[49,56,112]{2,1,0:T(8,128)(2,1)S(1)}, u32[]{:S(2)}, u32[]{:S(2)}) collective-permute-start(bf16[49,56,112]{2,1,0:T(8,128)(2,1)S(1)} %collective-permute-done.17.refs_4_), channel_id=1, source_target_pairs={{0,4},{1,5},{2,6},{3,7},{4,0},{5,1},{6,2},{7,3},{8,12},{9,13},{10,... | collective-permute-start | bytes 1843976 | tf_op jit(solution)/shard_map/ppermute | solution.py:429
  200.6 2.6 collective-permute-start.20
  222.4 20.2 %collective-permute-start.22 = (bf16[784,448]{1,0:T(8,128)(2,1)S(1)}, bf16[784,448]{1,0:T(8,128)(2,1)S(1)}, u32[]{:S(2)}, u32[]{:S(2)}) collective-permute-start(bf16[784,448]{1,0:T(8,128)(2,1)S(1)} %add_convert_fusion.1), channel_id=1, source_target_pairs={{0,2},{1,3},{2,0},{3,1},{4,6},{5,7},{6,4},{7,5},{8,10},{9,11},{10,... | collective-permute-start | bytes 2107400 | tf_op jit(solution)/shard_map/ppermute | solution.py:429
  247.6 4.3 %collective-permute-start.24 = (f32[128,128]{1,0:T(8,128)S(1)}, f32[128,128]{1,0:T(8,128)S(1)}, u32[]{:S(2)}, u32[]{:S(2)}) collective-permute-start(f32[128,128]{1,0:T(8,128)S(1)} %get-tuple-element.44), channel_id=1, source_target_pairs={{0,2},{1,3},{2,0},{3,1},{4,6},{5,7},{6,4},{7,5},{8,10},{9,11},{10,... | collective-permute-start | bytes 196616 | tf_op jit(solution)/shard_map/ppermute | solution.py:429
  249.2 5.0 %collective-permute-start.25 = (f32[128,128]{1,0:T(8,128)S(1)}, f32[128,128]{1,0:T(8,128)S(1)}, u32[]{:S(2)}, u32[]{:S(2)}) collective-permute-start(f32[128,128]{1,0:T(8,128)S(1)} %get-tuple-element.46), channel_id=1, source_target_pairs={{0,4},{1,5},{2,6},{3,7},{4,0},{5,1},{6,2},{7,3},{8,12},{9,13},{10,... | collective-permute-start | bytes 196616 | tf_op jit(solution)/shard_map/ppermute | solution.py:429
  249.7 5.2 %collective-permute-start.26 = (f32[128,128]{1,0:T(8,128)S(1)}, f32[128,128]{1,0:T(8,128)S(1)}, u32[]{:S(2)}, u32[]{:S(2)}) collective-permute-start(f32[128,128]{1,0:T(8,128)S(1)} %get-tuple-element.45), channel_id=1, source_target_pairs={{0,6},{1,7},{2,4},{3,5},{4,2},{5,3},{6,0},{7,1},{8,14},{9,15},{10,... | collective-permute-start | bytes 196616 | tf_op jit(solution)/shard_map/ppermute | solution.py:429
  254.9 5.5 %collective-permute-start.27 = (f32[128,128]{1,0:T(8,128)S(1)}, f32[128,128]{1,0:T(8,128)S(1)}, u32[]{:S(2)}, u32[]{:S(2)}) collective-permute-start(f32[128,128]{1,0:T(8,128)S(1)} %fusion.5), channel_id=1, source_target_pairs={{0,8},{1,9},{2,10},{3,11},{4,12},{5,13},{6,14},{7,15},{8,0},{9,1},... | collective-permute-start | bytes 196616 | tf_op jit(solution)/shard_map/ppermute | solution.py:429
  257.5 6.0 %collective-permute-start.28 = (f32[128,128]{1,0:T(8,128)S(1)}, f32[128,128]{1,0:T(8,128)S(1)}, u32[]{:S(2)}, u32[]{:S(2)}) collective-permute-start(f32[128,128]{1,0:T(8,128)S(1)} %fusion.5), channel_id=1, source_target_pairs={{0,16},{1,17},{2,18},{3,19},{4,20},{5,21},{6,22},{7,23},{8,24},{9,... | collective-permute-start | bytes 196616 | tf_op jit(solution)/shard_map/ppermute | solution.py:429
  258.6 6.2 %collective-permute-start.29 = (f32[128,128]{1,0:T(8,128)S(1)}, f32[128,128]{1,0:T(8,128)S(1)}, u32[]{:S(2)}, u32[]{:S(2)}) collective-permute-start(f32[128,128]{1,0:T(8,128)S(1)} %fusion.5), channel_id=1, source_target_pairs={{0,24},{1,25},{2,26},{3,27},{4,28},{5,29},{6,30},{7,31},{8,16},{9,... | collective-permute-start | bytes 196616 | tf_op jit(solution)/shard_map/ppermute | solution.py:429
  264.8 4.3 %collective-permute-start.30 = (f32[128,128]{1,0:T(8,128)S(1)}, f32[128,128]{1,0:T(8,128)S(1)}, u32[]{:S(2)}, u32[]{:S(2)}) collective-permute-start(f32[128,128]{1,0:T(8,128)S(1)} %add_add_fusion), channel_id=1, source_target_pairs={{0,2},{1,3},{2,0},{3,1},{4,6},{5,7},{6,4},{7,5},{8,10},{9,11},{10,... | collective-permute-start | bytes 196616 | tf_op jit(solution)/shard_map/ppermute | solution.py:429
  265.3 4.3 %collective-permute-start.31 = (f32[128,128]{1,0:T(8,128)S(1)}, f32[128,128]{1,0:T(8,128)S(1)}, u32[]{:S(2)}, u32[]{:S(2)}) collective-permute-start(f32[128,128]{1,0:T(8,128)S(1)} %add_add_fusion), channel_id=1, source_target_pairs={{0,4},{1,5},{2,6},{3,7},{4,0},{5,1},{6,2},{7,3},{8,12},{9,13},{10,... | collective-permute-start | bytes 196616 | tf_op jit(solution)/shard_map/ppermute | solution.py:429
  266.2 5.2 %collective-permute-start.32 = (f32[128,128]{1,0:T(8,128)S(1)}, f32[128,128]{1,0:T(8,128)S(1)}, u32[]{:S(2)}, u32[]{:S(2)}) collective-permute-start(f32[128,128]{1,0:T(8,128)S(1)} %add_add_fusion), channel_id=1, source_target_pairs={{0,6},{1,7},{2,4},{3,5},{4,2},{5,3},{6,0},{7,1},{8,14},{9,15},{10,... | collective-permute-start | bytes 196616 | tf_op jit(solution)/shard_map/ppermute | solution.py:429
  274.0 19.9 %collective-permute-start.34 = (bf16[784,448]{1,0:T(8,128)(2,1)S(1)}, bf16[784,448]{1,0:T(8,128)(2,1)S(1)}, u32[]{:S(2)}, u32[]{:S(2)}) collective-permute-start(bf16[784,448]{1,0:T(8,128)(2,1)S(1)} %add_convert_fusion.refs_0_), channel_id=1, source_target_pairs={{0,2},{1,3},{2,0},{3,1},{4,6},{5,7},{6,4},{7,5},{8,10},{9,11},{10,... | collective-permute-start | bytes 2107400 | tf_op jit(solution)/shard_map/ppermute | solution.py:429
  275.5 47.1 %collective-permute-start.35 = (bf16[784,448]{1,0:T(8,128)(2,1)S(1)}, bf16[784,448]{1,0:T(8,128)(2,1)S(1)}, u32[]{:S(2)}, u32[]{:S(2)}) collective-permute-start(bf16[784,448]{1,0:T(8,128)(2,1)S(1)} %add_convert_fusion.refs_0_), channel_id=1, source_target_pairs={{0,1},{1,0},{2,3},{3,2},{4,5},{5,4},{6,7},{7,6},{8,9},{9,8},{10,11... | collective-permute-start | bytes 2107400 | tf_op jit(solution)/shard_map/ppermute | solution.py:429
  293.9 28.6 %collective-permute-start.36 = (bf16[784,448]{1,0:T(8,128)(2,1)S(1)}, bf16[784,448]{1,0:T(8,128)(2,1)S(1)}, u32[]{:S(2)}, u32[]{:S(2)}) collective-permute-start(bf16[784,448]{1,0:T(8,128)(2,1)S(1)} %collective-permute-done.34.refs_1_), channel_id=1, source_target_pairs={{0,1},{1,0},{2,3},{3,2},{4,5},{5,4},{6,7},{7,6},{8,9},{9,8},{10,11... | collective-permute-start | bytes 2107400 | tf_op jit(solution)/shard_map/ppermute | solution.py:429
  (20 other events, 277.7 us)
